TPU v7x, 256 devices: a whole 4x4x8 slice. The times are simulated.
256 devices in a mesh: cluster: 4 (over x), sub: 64 (over y, z, core).
Axes of the slice: x: 4, y: 4, z: 8, core: 2. Of those that a mesh axis runs over, the one named last changes fastest.
Arguments:
- dual_ops: float32 [262144, 1024], P(('cluster', 'sub')), may hold values from -21 to 21, as said below
- boundary_solve_blocks: float32 [262144, 1024], P(('cluster', 'sub')), may hold values from -21 to 21, as said below
- rigid_images: float32 [1536, 1024], P(('cluster', 'sub')), may hold values from -0.1875 to 0.1875
- coarse_rows: float32 [1536, 1536], P(('cluster', 'sub')), may hold values from -1.5 to 1.5, as said below
- gap_raw: float32 [262144, 256], P(('cluster', 'sub')), may hold values from -12 to 12
- row_maps: int32 [256, 2, 128], P(('cluster', 'sub')), may hold values from 0 to 1023, as said below
Outputs:
- multipliers: float32 [262144, 256], P(('cluster', 'sub'))
- residual: float32 [262144, 256], P(('cluster', 'sub'))
- norms: float32 [2, 256], replicated
Inputs may be any that keep to these rules, and one draw needn't show every extreme that they name: `row_maps`: A subdomain's 2 * 128 row numbers all differ; its second list faces the first list of the next subdomain, row by row. `dual_ops`: each block of a subdomain is symmetric positive definite. `boundary_solve_blocks`: each block of a subdomain is symmetric positive definite. `coarse_rows`: Symmetric.
All inputs are finite; a program needn't handle non-finite values.
Results may differ from a plain program's by a relative error of at most 0.0003.
Values sent between devices are 32-bit elements; how exact they have to be, the bound alone decides.
No kernel may reach another device: no remote copies, remote signals or barrier semaphores. Data moves between devices by JAX's collectives and lax.ppermute only.
A program may use at most 64 MiB of HBM per device.

v0:
```python
import functools

import jax
import jax.numpy as jnp
from jax import lax
from jax.experimental import pallas as pl
from jax.experimental.pallas import tpu as pltpu
from jax.sharding import Mesh
from jax.sharding import PartitionSpec as P

CLUSTER_SUB = ("cluster", "sub_0", "sub_1", "sub_2")
OUTER = ("cluster", "sub_0")
INNER = ("sub_1", "sub_2")
TILE = 8
ROWS = 256
VMEM_LIMIT = 24 * 1024 * 1024

FULL = lax.Precision.HIGHEST
F32 = jnp.float32
BF16 = jnp.bfloat16


def dot(a, b, precision=FULL):
    return jnp.dot(a, b, precision=precision, preferred_element_type=F32)


def fast(a, b):
    return jnp.dot(a, b, preferred_element_type=F32)


def halves(value):
    high = value.astype(BF16)
    return high, (value - high.astype(F32)).astype(BF16)


def rounded_halves(value):
    high = lax.reduce_precision(value, exponent_bits=8, mantissa_bits=7)
    return high.astype(BF16), (value - high).astype(BF16)


def swap(blocks, axis):
    return lax.all_to_all(blocks, axis, split_axis=0, concat_axis=0, tiled=True)


def matched(value, pairs):
    return lax.ppermute(value, CLUSTER_SUB, pairs)


def matchings(count):
    near = [(i, i ^ 1) for i in range(count)]
    far = [(i, i if i in (0, count - 1) else ((i + 1) ^ 1) - 1) for i in range(count)]
    return near, far


def call(body, out_shapes, scratch, flops, moved):
    def run(*operands):
        return pl.pallas_call(
            body,
            out_shape=[jax.ShapeDtypeStruct(s, F32) for s in out_shapes],
            in_specs=[pl.BlockSpec(memory_space=pltpu.VMEM)] * len(operands),
            out_specs=[pl.BlockSpec(memory_space=pltpu.VMEM)] * len(out_shapes),
            scratch_shapes=scratch,
            compiler_params=pltpu.CompilerParams(vmem_limit_bytes=VMEM_LIMIT),
            cost_estimate=pl.CostEstimate(flops=flops, bytes_accessed=moved, transcendentals=0),
        )(*operands)

    return run


def summed(near_ref):
    total = near_ref[0]
    for member in range(1, near_ref.shape[0]):
        total = total + near_ref[member]
    return total


def stacked(amounts):
    spare = jnp.zeros((TILE, amounts.shape[1]), F32)
    high, low = halves(jnp.concatenate([amounts, spare], axis=0))
    return jnp.concatenate([high, low, high], axis=0)


def blocks_of(rows, body, start):
    return lax.fori_loop(0, rows // ROWS, lambda i, c: body(pl.ds(pl.multiple_of(i * ROWS, ROWS), ROWS), i, c), start)


def multiply(m_ref, s_ref, x_ref, high_ref, low_ref, out_ref, mate_ref, far_ref, part_ref):
    rows, cases = out_ref.shape
    shared = mate_ref.shape[0]
    xh, xl = high_ref[...], low_ref[...]

    def step(at, i, carry):
        part, sent = carry
        mh, ml = halves(m_ref[at, :])
        out = fast(mh, xh) + fast(mh, xl) + fast(ml, xh)
        out_ref[at, :] = out
        part = part + jnp.sum(x_ref[at, :] * out, axis=0, keepdims=True)
        uh, ul = halves(out)
        pick = s_ref[i]
        return part, sent + fast(pick, uh) + fast(pick, ul)

    start = (jnp.zeros((1, cases), F32), jnp.zeros((2 * shared, cases), F32))
    part, sent = blocks_of(rows, step, start)
    part_ref[...] = part
    mate_ref[...] = sent[:shared]
    far_ref[...] = sent[shared:]


def keep(at, x, x_ref, high_ref, low_ref):
    x_ref[at, :] = x
    high_ref[at, :], low_ref[at, :] = halves(x)


def precondition_first(near_ref, r_ref, w_ref, rt_ref, m_ref, s_ref,
                       out_ref, mate_ref, far_ref, part_ref, total_ref, x_ref, high_ref, low_ref):
    total = summed(near_ref)
    total_ref[...] = total
    amounts = stacked(total)

    def step(at, i, carry):
        keep(at, w_ref[at, :] * (r_ref[at, :] - fast(rt_ref[at, :], amounts)), x_ref, high_ref, low_ref)
        return carry

    blocks_of(r_ref.shape[0], step, 0)
    multiply(m_ref, s_ref, x_ref, high_ref, low_ref, out_ref, mate_ref, far_ref, part_ref)


def direct_first(near_ref, v_ref, rt_ref, m_ref, s_ref,
                 out_ref, mate_ref, far_ref, part_ref, total_ref, x_ref, high_ref, low_ref):
    total = summed(near_ref)
    total_ref[...] = total
    amounts = stacked(total)

    def step(at, i, carry):
        keep(at, v_ref[at, :] - fast(rt_ref[at, :], amounts), x_ref, high_ref, low_ref)
        return carry

    blocks_of(v_ref.shape[0], step, 0)
    multiply(m_ref, s_ref, x_ref, high_ref, low_ref, out_ref, mate_ref, far_ref, part_ref)


def precondition_next(modes, near_ref, before_ref, norm_ref, r_ref, image_ref, w_ref, rt_ref, m_ref, s_ref,
                      out_ref, mate_ref, far_ref, part_ref, size_ref, r_out_ref, step_ref, x_ref, high_ref, low_ref):
    total = summed(near_ref)
    length = norm_ref[modes:modes + 1, :] / total[modes:modes + 1]
    step_ref[...] = length
    amounts = stacked(before_ref[...] - length * total)

    def step(at, i, size):
        residual = r_ref[at, :] - length * image_ref[at, :]
        r_out_ref[at, :] = residual
        weighted = w_ref[at, :] * residual
        keep(at, w_ref[at, :] * (residual - fast(rt_ref[at, :], amounts)), x_ref, high_ref, low_ref)
        return size + jnp.sum(weighted * residual, axis=0, keepdims=True)

    size_ref[...] = blocks_of(r_ref.shape[0], step, jnp.zeros((1, r_ref.shape[1]), F32))
    multiply(m_ref, s_ref, x_ref, high_ref, low_ref, out_ref, mate_ref, far_ref, part_ref)


def direct_next(modes, near_ref, norm_ref, v_ref, d_ref, rt_ref, m_ref, s_ref,
                out_ref, mate_ref, far_ref, part_ref, total_ref, x_ref, high_ref, low_ref):
    total = summed(near_ref)
    total_ref[...] = total
    ratio = total[modes:modes + 1] / norm_ref[modes:modes + 1, :]
    amounts = stacked(total)

    def step(at, i, carry):
        update = v_ref[at, :] - fast(rt_ref[at, :], amounts)
        keep(at, update + ratio * d_ref[at, :], x_ref, high_ref, low_ref)
        return carry

    blocks_of(v_ref.shape[0], step, 0)
    multiply(m_ref, s_ref, x_ref, high_ref, low_ref, out_ref, mate_ref, far_ref, part_ref)


def received(mate_ref, far_ref):
    return halves(jnp.concatenate([mate_ref[...], far_ref[...]], axis=0))


def pack_out(modes, pack_ref, sums, low_sums, first, second):
    part = sums[:TILE] + sums[TILE:] + low_sums[:TILE]
    row = lax.broadcasted_iota(jnp.int32, part.shape, 0)
    part = jnp.where(row == modes, first, jnp.where(row == modes + 1, second, part))
    for member in range(pack_ref.shape[0]):
        pack_ref[member] = part


def gather_modes(rigid_ref, value, i, sums, low_sums):
    zh, zl = halves(value)
    rigid = rigid_ref[i]
    return sums + fast(rigid, zh), low_sums + fast(rigid, zl)


def start_body(modes, y_ref, mate_ref, far_ref, st_ref, w_ref, rigid_ref, out_ref, pack_ref):
    rh, rl = received(mate_ref, far_ref)
    cases = y_ref.shape[1]

    def step(at, i, carry):
        size, sums, low_sums = carry
        place = st_ref[at, :]
        value = y_ref[at, :] + (fast(place, rh) + fast(place, rl))
        out_ref[at, :] = value
        size = size + jnp.sum(w_ref[at, :] * value * value, axis=0, keepdims=True)
        return (size, *gather_modes(rigid_ref, value, i, sums, low_sums))

    zeros = jnp.zeros((2 * TILE, cases), F32)
    size, sums, low_sums = blocks_of(y_ref.shape[0], step, (jnp.zeros((1, cases), F32), zeros, zeros))
    pack_out(modes, pack_ref, sums, low_sums, size, jnp.zeros_like(size))


def assemble_body(modes, weighted, sized, *refs):
    y_ref, mate_ref, far_ref, st_ref, rigid_ref, part_ref = refs[:6]
    w_ref = refs[6] if weighted else None
    size_ref = refs[6 + weighted] if sized else None
    out_ref, pack_ref = refs[6 + weighted + sized:]
    rh, rl = received(mate_ref, far_ref)

    def step(at, i, carry):
        place = st_ref[at, :]
        value = y_ref[at, :] + (fast(place, rh) + fast(place, rl))
        if weighted:
            value = w_ref[at, :] * value
        out_ref[at, :] = value
        return gather_modes(rigid_ref, value, i, *carry)

    zeros = jnp.zeros((2 * TILE, y_ref.shape[1]), F32)
    sums, low_sums = blocks_of(y_ref.shape[0], step, (zeros, zeros))
    part = part_ref[...]
    pack_out(modes, pack_ref, sums, low_sums, part, size_ref[...] if sized else jnp.zeros_like(part))


def block_body(block_ref, near_ref, out_ref):
    members, tile, cases = near_ref.shape
    high, low = halves(near_ref[...].reshape(members * tile, cases))
    out = fast(block_ref[...], jnp.concatenate([high, low, high], axis=0))
    out_ref[...] = out.reshape(out_ref.shape)


def finish_body(q_ref, mate_ref, far_ref, st_ref, r_ref, first_ref, second_ref, step_first_ref, step_ref,
                multipliers_ref, residual_ref):
    rh, rl = received(mate_ref, far_ref)
    first, second = step_first_ref[...], step_ref[...]

    def step(at, i, carry):
        place = st_ref[at, :]
        image = q_ref[at, :] + (fast(place, rh) + fast(place, rl))
        multipliers_ref[at, :] = first * first_ref[at, :] + second * second_ref[at, :]
        residual_ref[at, :] = r_ref[at, :] - second * image
        return carry

    blocks_of(q_ref.shape[0], step, 0)


def shards(dual_ops, boundary_solve_blocks, rigid_images, coarse_rows, gap_raw, row_maps):
    modes, local_rows = rigid_images.shape
    cases = gap_raw.shape[1]
    count = lax.axis_size(CLUSTER_SUB)
    outer, inner = lax.axis_size(OUTER), lax.axis_size(INNER)
    place = lax.axis_index(CLUSTER_SUB)
    even = place % 2 == 0
    inside = jnp.where((place > 0) & (place < count - 1), 1.0, 0.0).astype(F32)
    mate = jnp.where(even, row_maps[0, 1], row_maps[0, 0])
    far = jnp.where(even, row_maps[0, 0], row_maps[0, 1])
    shared = mate.shape[0]
    mate_pairs, far_pairs = matchings(count)

    def exchanged(to_mate, to_far):
        from_far = matched(to_far, far_pairs)
        from_mate = matched(to_mate, mate_pairs)
        return from_mate, from_far

    gap_near = exchanged(gap_raw[mate], gap_raw[far])

    picks = jnp.concatenate([mate, far])
    live = jnp.concatenate([jnp.ones((shared,), F32), jnp.full((shared,), inside)])
    one_hot = jnp.where(
        picks[:, None] == lax.broadcasted_iota(jnp.int32, (2 * shared, local_rows), 1), live[:, None], 0.0
    )
    selector = one_hot.astype(BF16).reshape(2 * shared, local_rows // ROWS, ROWS).transpose(1, 0, 2)
    placer = jnp.where(
        picks[None, :] == lax.broadcasted_iota(jnp.int32, (local_rows, 2 * shared), 0), live[None, :], 0.0
    )
    weights = jnp.broadcast_to(1.0 - 0.5 * jnp.sum(placer, axis=1, keepdims=True), (local_rows, cases))
    placer = placer.astype(BF16)

    rigid_shared = lax.dot_general(
        rigid_images, one_hot, (((1,), (1,)), ((), ())), precision=FULL, preferred_element_type=F32
    )
    from_mate, from_far = exchanged(
        jnp.concatenate([coarse_rows, rigid_shared[:, :shared]], axis=1),
        jnp.concatenate([coarse_rows, rigid_shared[:, shared:]], axis=1),
    )
    order = coarse_rows.shape[1]

    def across(near, hot):
        return lax.dot_general(
            hot, near, (((0,), (1,)), ((), ())), precision=FULL, preferred_element_type=F32
        )

    gap = jnp.zeros((local_rows, TILE - modes), F32)
    rigid_tall = jnp.concatenate(
        [
            rigid_images.T,
            gap,
            across(from_mate[:, order:], one_hot[:shared]),
            gap,
            across(from_far[:, order:], one_hot[shared:]),
            gap,
            jnp.zeros((local_rows, TILE), F32),
        ],
        axis=1,
    )
    tall_high, tall_low = rounded_halves(rigid_tall)
    rigid_tall = jnp.concatenate([tall_high, tall_high, tall_low], axis=1)
    wide_high, wide_low = rounded_halves(jnp.pad(rigid_images, ((0, TILE - modes), (0, 0))))
    rigid_wide = jnp.concatenate([wide_high, wide_low], axis=0)
    rigid_wide = rigid_wide.reshape(2 * TILE, local_rows // ROWS, ROWS).transpose(1, 0, 2)

    rows_here = jnp.concatenate([coarse_rows, from_mate[:, :order], from_far[:, :order]], axis=0)
    block = swap(rows_here.reshape(3 * modes, outer, inner * modes).transpose(1, 0, 2), OUTER)
    block = jnp.pad(
        block.reshape(outer, 3, modes, inner, modes),
        ((0, 0), (0, 0), (0, TILE - modes), (0, 0), (0, TILE - modes)),
    )
    shape = (1, 3, TILE, 1, TILE)
    part_of = lax.broadcasted_iota(jnp.int32, shape, 1)
    tile_row = lax.broadcasted_iota(jnp.int32, shape, 2)
    tile_col = lax.broadcasted_iota(jnp.int32, shape, 4)
    sums = ((part_of == 0) & (tile_row == tile_col) & (tile_row >= modes)).astype(F32)
    block_high, block_low = rounded_halves((block + sums).reshape(outer * 3 * TILE, inner * TILE))
    block = jnp.concatenate([block_high, block_high, block_low], axis=1)

    field = (local_rows, cases)
    edge = (shared, cases)
    row = (1, cases)
    rows_out = (3 * TILE, cases)
    pack_shape = (inner, TILE, cases)
    scratch = [pltpu.VMEM(field, F32), pltpu.VMEM(field, BF16), pltpu.VMEM(field, BF16)]
    own = scratch[1:]
    big = 6 * local_rows * local_rows * cases
    light = 4 * local_rows * cases * 2 * shared
    moved = 4 * local_rows * (local_rows + 3 * cases)

    def coarse(pack):
        near = swap(pack, INNER)
        [rows] = call(block_body, [(outer, 3 * TILE, cases)], [], 6 * block.shape[0] * block.shape[1] * cases,
                      4 * outer * 4 * TILE * cases)(block, near)
        return swap(rows, OUTER)

    def assemble(weighted, sized, *operands):
        body = functools.partial(assemble_body, modes, weighted, sized)
        return call(body, [field, pack_shape], [], light, 12 * local_rows * cases)(*operands)

    residual, pack = call(functools.partial(start_body, modes), [field, pack_shape], [], light, 12 * local_rows * cases)(
        gap_raw, *gap_near, placer, weights, rigid_wide
    )
    near = coarse(pack)
    out, to_mate, to_far, part, amounts = call(
        precondition_first, [field, edge, edge, row, rows_out], scratch, big, moved
    )(near, residual, weights, rigid_tall, boundary_solve_blocks, selector)
    norm_first = amounts[modes]
    smoothed, pack = assemble(True, False, out, *exchanged(to_mate, to_far), placer, rigid_wide, part, weights)
    near = coarse(pack)
    out, to_mate, to_far, part, total, direction_first = call(
        direct_first, [field, edge, edge, row, rows_out, field], own, big, moved
    )(near, smoothed, rigid_tall, dual_ops, selector)
    image, pack = assemble(False, False, out, *exchanged(to_mate, to_far), placer, rigid_wide, part)
    near = coarse(pack)
    out, to_mate, to_far, part, size, residual, step_first = call(
        functools.partial(precondition_next, modes), [field, edge, edge, row, row, field, row], scratch, big, moved
    )(near, amounts, total, residual, image, weights, rigid_tall, boundary_solve_blocks, selector)
    smoothed, pack = assemble(True, True, out, *exchanged(to_mate, to_far), placer, rigid_wide, part, weights, size)
    near = coarse(pack)
    out, to_mate, to_far, part, last, direction = call(
        functools.partial(direct_next, modes), [field, edge, edge, row, rows_out, field], own, big, moved
    )(near, total, smoothed, direction_first, rigid_tall, dual_ops, selector)
    norm_second = last[modes + 1]
    from_mate, from_far = exchanged(to_mate, to_far)
    bending = jnp.sum(swap(jnp.broadcast_to(part, (count, 1, cases)), CLUSTER_SUB), axis=0)
    step = last[modes:modes + 1] / bending
    multipliers, residual = call(finish_body, [field, field], [], light, 24 * local_rows * cases)(
        out, from_mate, from_far, placer, residual, direction_first, direction, step_first, step
    )
    return (multipliers, residual, jnp.stack([norm_first, norm_second]))


def solution(mesh):
    devices = mesh.devices
    x, sub = devices.shape
    split = Mesh(devices.reshape(x, 4, sub // 8, 2), CLUSTER_SUB)
    in_specs = (P(CLUSTER_SUB, None),) * 5 + (P(CLUSTER_SUB, None, None),)
    out_specs = (P(CLUSTER_SUB, None), P(CLUSTER_SUB, None), P())
    return jax.shard_map(
        shards, mesh=split, in_specs=in_specs, out_specs=out_specs, check_vma=False
    )
```

profile of v0, /device:TPU:1, one launch (start us, length us, event | category | flops | bytes accessed | tf_op | source)
XLA Modules:
  0.0 248.0 jit_solution(3580656806404407378)
XLA Ops:
  0.7 0.8 fusion.13
  1.5 1.8 convolution_bitcast_fusion
  3.3 1.5 pad_maximum_fusion.3
  4.7 4.9 %collective-permute-start.1 = (f32[6,1664]{1,0:T(8,128)}, f32[6,1664]{1,0:T(8,128)}, u32[]{:S(2)}, u32[]{:S(2)}) collective-permute-start(f32[6,1664]{1,0:T(8,128)} %get-tuple-element.80), channel_id=1, source_target_pairs={{0,0},{1,2},{2,1},{3,4},{4,3},{5,6},{6,5},{7,8},{8,7},{9,10},{10,9... | collective-permute-start | bytes 119816 | tf_op jit(solution)/shard_map/ppermute | solution.py:46
  10.0 1.4 gather_fusion
  11.7 1.4 gather_fusion.1
  13.1 3.4 %collective-permute-start.3 = (f32[128,256]{1,0:T(8,128)}, f32[128,256]{1,0:T(8,128)S(1)}, u32[]{:S(2)}, u32[]{:S(2)}) collective-permute-start(f32[128,256]{1,0:T(8,128)} %gather_fusion.1), channel_id=1, source_target_pairs={{0,0},{1,2},{2,1},{3,4},{4,3},{5,6},{6,5},{7,8},{8,7},{9,10},{10,9... | collective-permute-start | bytes 393224 | tf_op jit(solution)/shard_map/ppermute | solution.py:46
  17.5 0.8 slice.59
  18.3 0.8 slice.61
  19.1 0.7 pad_maximum_fusion.2
  19.8 1.7 reshape.121
  21.4 1.6 copy.43
  23.1 8.6 %all-to-all-start = ((f32[16,18,96]{2,1,0:T(8,128)}), f32[16,18,96]{2,1,0:T(8,128)}, u32[]{:S(2)}, u32[]{:S(2)}) async-start(f32[16,18,96]{2,1,0:T(8,128)} %copy.43), calls=%async_computation | async-start | bytes 393216 | tf_op jit(solution)/shard_map/all_to_all | solution.py:42
  31.6 1.1 fusion.1
  32.7 1.1 fusion.3
  33.9 1.0 copy.48
  34.9 1.0 copy.47
  36.1 1.8 shard_map.85
  37.9 1.0 copy-done.4
  38.9 0.7 copy-done.17
  39.5 7.5 %all-to-all-start.1 = ((f32[16,8,256]{2,1,0:T(8,128)}), f32[16,8,256]{2,1,0:T(8,128)S(1)}, u32[]{:S(2)}, u32[]{:S(2)}) async-start(f32[16,8,256]{2,1,0:T(8,128)} %copy-done.17), calls=%async_computation.1 | async-start | bytes 262144 | tf_op jit(solution)/shard_map/all_to_all | solution.py:42
  47.1 2.1 copy.44
  49.2 2.3 reshape.122
  51.6 2.6 %pad_add_fusion = f32[16,3,8,16,8]{0,4,3,2,1:T(8,128)} fusion(f32[16,3,6,16,6]{0,4,3,2,1:T(8,128)} %reshape.122, f32[3,8,8]{2,1,0:T(8,128)S(1)} %fusion.10), kind=kLoop, calls=%fused_computation.2 | loop fusion | flops 49152 | bytes 307968 | tf_op jit(solution)/shard_map/add | solution.py:330
  54.2 4.6 %copy.45 = f32[16,3,8,16,8]{4,3,2,1,0:T(8,128)} copy(f32[16,3,8,16,8]{0,4,3,2,1:T(8,128)} %pad_add_fusion) | data formatting | bytes 393216 | tf_op jit(solution)/shard_map/add | solution.py:330
  58.8 3.0 %reshape.123 = f32[384,128]{1,0:T(8,128)S(1)} reshape(f32[16,3,8,16,8]{4,3,2,1,0:T(8,128)} %copy.45) | data formatting | bytes 393216 | tf_op jit(solution)/shard_map/reshape | solution.py:330
  62.2 0.7 copy-done.14
  62.9 0.7 copy-done.15
  63.7 6.8 %all-to-all-start.2 = ((f32[16,24,256]{2,1,0:T(8,128)}), f32[16,24,256]{2,1,0:T(8,128)}, u32[]{:S(2)}, u32[]{:S(2)}) async-start(f32[16,24,256]{2,1,0:T(8,128)} %copy-done.14), calls=%async_computation.2 | async-start | bytes 786432 | tf_op jit(solution)/shard_map/all_to_all | solution.py:42
  70.5 1.5 fusion.16
  72.2 7.5 %all-to-all-done.2.near_ref = f32[16,24,256]{2,1,0:T(8,128)} async-done(((f32[16,24,256]{2,1,0:T(8,128)}), f32[16,24,256]{2,1,0:T(8,128)}, u32[]{:S(2)}, u32[]{:S(2)}) %all-to-all-start.2) | async-done | bytes 393248 | tf_op jit(solution)/shard_map/all_to_all | solution.py:42
  79.7 2.2 copy-done
  81.9 5.6 %shard_map.87 = (f32[1024,256]{1,0:T(8,128)S(1)}, f32[128,256]{1,0:T(8,128)S(1)}, f32[128,256]{1,0:T(8,128)S(1)}, f32[1,256]{1,0:T(1,128)S(1)}, f32[24,256]{1,0:T(8,128)S(1)}) custom-call(f32[16,24,256]{2,1,0:T(8,128)} %all-to-all-done.2.near_ref, f32[1024,256]{1,0:T(8,128)S(1)} %copy-done.5, f32[1024,256]{1,0:T(8,128)S(1)} %broadcast_in_dim.58.w_ref.refs_6_, ...), custom_call_target="tpu_custom_call" | custom-call | flops 1610612736 | bytes 7340032 | tf_op jit(solution)/shard_map/pallas_call | solution.py:57
  87.5 1.7 collective-permute-start.4
  89.2 3.2 %collective-permute-start.5 = (f32[128,256]{1,0:T(8,128)S(1)}, f32[128,256]{1,0:T(8,128)S(1)}, u32[]{:S(2)}, u32[]{:S(2)}) collective-permute-start(f32[128,256]{1,0:T(8,128)S(1)} %get-tuple-element.41), channel_id=1, source_target_pairs={{0,0},{1,2},{2,1},{3,4},{4,3},{5,6},{6,5},{7,8},{8,7},{9,10},{10,9... | collective-permute-start | bytes 393224 | tf_op jit(solution)/shard_map/ppermute | solution.py:46
  92.4 3.1 %collective-permute-done.5.refs_2_ = f32[128,256]{1,0:T(8,128)S(1)} collective-permute-done((f32[128,256]{1,0:T(8,128)S(1)}, f32[128,256]{1,0:T(8,128)S(1)}, u32[]{:S(2)}, u32[]{:S(2)}) %collective-permute-start.5) | collective-permute-done | bytes 131104 | tf_op jit(solution)/shard_map/ppermute | solution.py:46
  95.5 1.8 shard_map.88
  97.2 16.7 %all_to_all.50.near_ref = f32[16,8,256]{2,1,0:T(8,128)S(1)} all-to-all(f32[16,8,256]{2,1,0:T(8,128)S(1)} %get-tuple-element.43), channel_id=1, replica_groups=mesh['cluster'=4,'sub_0'=4,'sub_1'=8,'sub_2'=2] {'sub_1','sub_2'}, dimensions={0} | all-to-all | bytes 262144 | tf_op jit(solution)/shard_map/all_to_all | solution.py:42
  114.3 12.3 %all_to_all.51.near_ref = f32[16,24,256]{2,1,0:T(8,128)S(1)} all-to-all(f32[16,24,256]{2,1,0:T(8,128)S(1)} %shard_map.89), channel_id=1, replica_groups=mesh['cluster'=4,'sub_0'=4,'sub_1'=8,'sub_2'=2] {'cluster','sub_0'}, dimensions={0} | all-to-all | bytes 786432 | tf_op jit(solution)/shard_map/all_to_all | solution.py:42
  126.5 4.6 %shard_map.90 = (f32[1024,256]{1,0:T(8,128)S(1)}, f32[128,256]{1,0:T(8,128)S(1)}, f32[128,256]{1,0:T(8,128)S(1)}, f32[1,256]{1,0:T(1,128)S(1)}, f32[24,256]{1,0:T(8,128)S(1)}, /*index=5*/f32[1024,256]{1,0:T(8,128)S(1)}) custom-call(f32[16,24,256]{2,1,0:T(8,128)S(1)} %all_to_all.51.near_ref, f32[1024,256]{1,0:T(8,128)S(1)} %get-tuple-element.44.v_ref, ...), custom_call_target="tpu_custom_call" | custom-call | flops 1610612736 | bytes 7340032 | tf_op jit(solution)/shard_map/pallas_call | solution.py:57
  131.2 1.8 collective-permute-start.6
  133.0 2.1 collective-permute-start.7
  135.1 4.1 %collective-permute-done.7.refs_2_ = f32[128,256]{1,0:T(8,128)S(1)} collective-permute-done((f32[128,256]{1,0:T(8,128)S(1)}, f32[128,256]{1,0:T(8,128)S(1)}, u32[]{:S(2)}, u32[]{:S(2)}) %collective-permute-start.7) | collective-permute-done | bytes 131104 | tf_op jit(solution)/shard_map/ppermute | solution.py:46
  139.2 1.8 shard_map.91
  141.0 12.6 %all_to_all.52.near_ref = f32[16,8,256]{2,1,0:T(8,128)S(1)} all-to-all(f32[16,8,256]{2,1,0:T(8,128)S(1)} %get-tuple-element.49), channel_id=1, replica_groups=mesh['cluster'=4,'sub_0'=4,'sub_1'=8,'sub_2'=2] {'sub_1','sub_2'}, dimensions={0} | all-to-all | bytes 262144 | tf_op jit(solution)/shard_map/all_to_all | solution.py:42
  153.9 14.8 %all_to_all.53.near_ref = f32[16,24,256]{2,1,0:T(8,128)S(1)} all-to-all(f32[16,24,256]{2,1,0:T(8,128)S(1)} %shard_map.92), channel_id=1, replica_groups=mesh['cluster'=4,'sub_0'=4,'sub_1'=8,'sub_2'=2] {'cluster','sub_0'}, dimensions={0} | all-to-all | bytes 786432 | tf_op jit(solution)/shard_map/all_to_all | solution.py:42
  168.7 4.7 %shard_map.93 = (f32[1024,256]{1,0:T(8,128)S(1)}, f32[128,256]{1,0:T(8,128)S(1)}, f32[128,256]{1,0:T(8,128)S(1)}, f32[1,256]{1,0:T(1,128)S(1)}, f32[1,256]{1,0:T...) custom-call(f32[16,24,256]{2,1,0:T(8,128)S(1)} %all_to_all.53.near_ref, ...), custom_call_target="tpu_custom_call" | custom-call | flops 1610612736 | bytes 7340032 | tf_op jit(solution)/shard_map/pallas_call | solution.py:57
  173.4 1.7 collective-permute-start.8
  175.1 1.9 collective-permute-start.9
  177.1 4.3 %collective-permute-done.9.refs_2_ = f32[128,256]{1,0:T(8,128)S(1)} collective-permute-done((f32[128,256]{1,0:T(8,128)S(1)}, f32[128,256]{1,0:T(8,128)S(1)}, u32[]{:S(2)}, u32[]{:S(2)}) %collective-permute-start.9) | collective-permute-done | bytes 131104 | tf_op jit(solution)/shard_map/ppermute | solution.py:46
  181.4 1.8 shard_map.94
  183.2 12.2 %all_to_all.54.near_ref = f32[16,8,256]{2,1,0:T(8,128)S(1)} all-to-all(f32[16,8,256]{2,1,0:T(8,128)S(1)} %get-tuple-element.58), channel_id=1, replica_groups=mesh['cluster'=4,'sub_0'=4,'sub_1'=8,'sub_2'=2] {'sub_1','sub_2'}, dimensions={0} | all-to-all | bytes 262144 | tf_op jit(solution)/shard_map/all_to_all | solution.py:42
  195.6 15.1 %all_to_all.55.near_ref = f32[16,24,256]{2,1,0:T(8,128)S(1)} all-to-all(f32[16,24,256]{2,1,0:T(8,128)S(1)} %shard_map.95), channel_id=1, replica_groups=mesh['cluster'=4,'sub_0'=4,'sub_1'=8,'sub_2'=2] {'cluster','sub_0'}, dimensions={0} | all-to-all | bytes 786432 | tf_op jit(solution)/shard_map/all_to_all | solution.py:42
  210.7 4.7 %shard_map.96 = (f32[1024,256]{1,0:T(8,128)S(1)}, f32[128,256]{1,0:T(8,128)S(1)}, f32[128,256]{1,0:T(8,128)S(1)}, f32[1,256]{1,0:T(1,128)S(1)}, f32[24,256]{1,0:T(8,128)S(1)}, /*index=5*/f32[1024,256]{1,0:T(8,128)S(1)}) custom-call(f32[16,24,256]{2,1,0:T(8,128)S(1)} %all_to_all.55.near_ref, f32[24,256]{1,0:T(8,128)S(1)} %get-tuple-element.51.norm_ref, ...), custom_call_target="tpu_custom_call" | custom-call | flops 1610612736 | bytes 7340032 | tf_op jit(solution)/shard_map/pallas_call | solution.py:57
  215.4 1.0 copy-done.10
  216.3 1.0 copy-done.12
  218.6 0.9 broadcast_in_dim.63
  219.5 6.6 %all-to-all-start.9 = ((f32[256,1,256]{2,1,0:T(1,128)}), f32[256,1,256]{2,1,0:T(1,128)S(1)}, u32[]{:S(2)}, u32[]{:S(2)}) async-start(f32[256,1,256]{2,1,0:T(1,128)} %broadcast_in_dim.63), calls=%async_computation.9 | async-start | bytes 524288 | tf_op jit(solution)/shard_map/all_to_all | solution.py:42
  226.1 2.4 collective-permute-start.10
  228.5 1.9 collective-permute-start.11
  230.4 12.0 %all-to-all-done.9 = f32[256,1,256]{2,1,0:T(1,128)S(1)} async-done(((f32[256,1,256]{2,1,0:T(1,128)}), f32[256,1,256]{2,1,0:T(1,128)S(1)}, u32[]{:S(2)}, u32[]{:S(2)}) %all-to-all-start.9) | async-done | bytes 262176 | tf_op jit(solution)/shard_map/all_to_all | solution.py:42
  243.3 1.2 copy-done.11
  244.5 1.2 copy-done.13
  245.7 2.3 shard_map.97
  (82 shorter events, 5.4 us)
Async XLA Ops:
  0.6 9.4 %copy-start.3 = (f32[1024,256]{1,0:T(8,128)S(1)}, f32[1024,256]{1,0:T(8,128)}, u32[]{:S(2)}) copy-start(f32[1024,256]{1,0:T(8,128)} %y_ref.1) | copy-start | bytes 3145732
  4.7 13.5 %collective-permute-start.1 = (f32[6,1664]{1,0:T(8,128)}, f32[6,1664]{1,0:T(8,128)}, u32[]{:S(2)}, u32[]{:S(2)}) collective-permute-start(f32[6,1664]{1,0:T(8,128)} %get-tuple-element.80), channel_id=1, source_target_pairs={{0,0},{1,2},{2,1},{3,4},{4,3},{5,6},{6,5},{7,8},{8,7},{9,10},{10,9... | collective-permute-start | bytes 119816 | tf_op jit(solution)/shard_map/ppermute | solution.py:46
  9.7 7.8 %collective-permute-start = (f32[6,1664]{1,0:T(8,128)}, f32[6,1664]{1,0:T(8,128)}, u32[]{:S(2)}, u32[]{:S(2)}) collective-permute-start(f32[6,1664]{1,0:T(8,128)} %get-tuple-element.79), channel_id=1, source_target_pairs={{0,1},{1,0},{2,3},{3,2},{4,5},{5,4},{6,7},{7,6},{8,9},{9,8},{10,11... | collective-permute-start | bytes 119816 | tf_op jit(solution)/shard_map/ppermute | solution.py:46
  11.4 5.7 %copy-start.21 = (f32[6,1024]{1,0:T(8,128)S(1)}, f32[6,1024]{1,0:T(8,128)}, u32[]{:S(2)}) copy-start(f32[6,1024]{1,0:T(8,128)} %param.8) | copy-start | bytes 73732
  11.4 24.5 %collective-permute-start.2 = (f32[128,256]{1,0:T(8,128)}, f32[128,256]{1,0:T(8,128)S(1)}, u32[]{:S(2)}, u32[]{:S(2)}) collective-permute-start(f32[128,256]{1,0:T(8,128)} %gather_fusion), channel_id=1, source_target_pairs={{0,1},{1,0},{2,3},{3,2},{4,5},{5,4},{6,7},{7,6},{8,9},{9,8},{10,11... | collective-permute-start | bytes 393224 | tf_op jit(solution)/shard_map/ppermute | solution.py:46
  11.7 7.4 %copy-start.20 = (f32[6,1536]{1,0:T(8,128)S(1)}, f32[6,1536]{1,0:T(8,128)}, u32[]{:S(2)}) copy-start(f32[6,1536]{1,0:T(8,128)} %param.9) | copy-start | bytes 110596
  13.1 22.8 %collective-permute-start.3 = (f32[128,256]{1,0:T(8,128)}, f32[128,256]{1,0:T(8,128)S(1)}, u32[]{:S(2)}, u32[]{:S(2)}) collective-permute-start(f32[128,256]{1,0:T(8,128)} %gather_fusion.1), channel_id=1, source_target_pairs={{0,0},{1,2},{2,1},{3,4},{4,3},{5,6},{6,5},{7,8},{8,7},{9,10},{10,9... | collective-permute-start | bytes 393224 | tf_op jit(solution)/shard_map/ppermute | solution.py:46
  23.1 16.5 %all-to-all-start = ((f32[16,18,96]{2,1,0:T(8,128)}), f32[16,18,96]{2,1,0:T(8,128)}, u32[]{:S(2)}, u32[]{:S(2)}) async-start(f32[16,18,96]{2,1,0:T(8,128)} %copy.43), calls=%async_computation | async-start | bytes 393216 | tf_op jit(solution)/shard_map/all_to_all | solution.py:42
  37.9 1.0 copy-start.4
  38.9 0.7 copy-start.17
  39.5 22.4 %all-to-all-start.1 = ((f32[16,8,256]{2,1,0:T(8,128)}), f32[16,8,256]{2,1,0:T(8,128)S(1)}, u32[]{:S(2)}, u32[]{:S(2)}) async-start(f32[16,8,256]{2,1,0:T(8,128)} %copy-done.17), calls=%async_computation.1 | async-start | bytes 262144 | tf_op jit(solution)/shard_map/all_to_all | solution.py:42
  62.2 0.7 copy-start.14
  62.9 0.7 copy-start.15
  63.7 16.0 %copy-start.5 = (f32[1024,256]{1,0:T(8,128)S(1)}, f32[1024,256]{1,0:T(8,128)}, u32[]{:S(2)}) copy-start(f32[1024,256]{1,0:T(8,128)} %copy-done.4) | copy-start | bytes 3145732
  63.7 16.0 %all-to-all-start.2 = ((f32[16,24,256]{2,1,0:T(8,128)}), f32[16,24,256]{2,1,0:T(8,128)}, u32[]{:S(2)}, u32[]{:S(2)}) async-start(f32[16,24,256]{2,1,0:T(8,128)} %copy-done.14), calls=%async_computation.2 | async-start | bytes 786432 | tf_op jit(solution)/shard_map/all_to_all | solution.py:42
  79.7 2.2 copy-start
  81.9 32.1 %copy-start.16 = (bf16[384,384]{1,0:T(8,128)(2,1)S(1)}, bf16[384,384]{1,0:T(8,128)(2,1)}, u32[]{:S(2)}) copy-start(bf16[384,384]{1,0:T(8,128)(2,1)} %copy-done.15) | copy-start | bytes 884740
  87.5 4.8 %collective-permute-start.4 = (f32[128,256]{1,0:T(8,128)S(1)}, f32[128,256]{1,0:T(8,128)S(1)}, u32[]{:S(2)}, u32[]{:S(2)}) collective-permute-start(f32[128,256]{1,0:T(8,128)S(1)} %get-tuple-element.40), channel_id=1, source_target_pairs={{0,1},{1,0},{2,3},{3,2},{4,5},{5,4},{6,7},{7,6},{8,9},{9,8},{10,11... | collective-permute-start | bytes 393224 | tf_op jit(solution)/shard_map/ppermute | solution.py:46
  89.2 6.3 %collective-permute-start.5 = (f32[128,256]{1,0:T(8,128)S(1)}, f32[128,256]{1,0:T(8,128)S(1)}, u32[]{:S(2)}, u32[]{:S(2)}) collective-permute-start(f32[128,256]{1,0:T(8,128)S(1)} %get-tuple-element.41), channel_id=1, source_target_pairs={{0,0},{1,2},{2,1},{3,4},{4,3},{5,6},{6,5},{7,8},{8,7},{9,10},{10,9... | collective-permute-start | bytes 393224 | tf_op jit(solution)/shard_map/ppermute | solution.py:46
  95.5 31.1 %copy-start.2 = (f32[1024,1024]{1,0:T(8,128)S(1)}, f32[1024,1024]{1,0:T(8,128)}, u32[]{:S(2)}) copy-start(f32[1024,1024]{1,0:T(8,128)} %m_ref.7) | copy-start | bytes 12582916
  126.5 42.2 %copy-start.1 = (f32[1024,1024]{1,0:T(8,128)S(1)}, f32[1024,1024]{1,0:T(8,128)}, u32[]{:S(2)}) copy-start(f32[1024,1024]{1,0:T(8,128)} %m_ref.6) | copy-start | bytes 12582916
  131.2 79.5 %copy-start.6 = (f32[1024,256]{1,0:T(8,128)}, f32[1024,256]{1,0:T(8,128)S(1)}, u32[]{:S(2)}) copy-start(f32[1024,256]{1,0:T(8,128)S(1)} %get-tuple-element.60.d_ref.first_ref) | copy-start | bytes 3145732
  131.2 3.9 %collective-permute-start.6 = (f32[128,256]{1,0:T(8,128)S(1)}, f32[128,256]{1,0:T(8,128)S(1)}, u32[]{:S(2)}, u32[]{:S(2)}) collective-permute-start(f32[128,256]{1,0:T(8,128)S(1)} %get-tuple-element.46), channel_id=1, source_target_pairs={{0,1},{1,0},{2,3},{3,2},{4,5},{5,4},{6,7},{7,6},{8,9},{9,8},{10,11... | collective-permute-start | bytes 393224 | tf_op jit(solution)/shard_map/ppermute | solution.py:46
  133.0 6.3 %collective-permute-start.7 = (f32[128,256]{1,0:T(8,128)S(1)}, f32[128,256]{1,0:T(8,128)S(1)}, u32[]{:S(2)}, u32[]{:S(2)}) collective-permute-start(f32[128,256]{1,0:T(8,128)S(1)} %get-tuple-element.47), channel_id=1, source_target_pairs={{0,0},{1,2},{2,1},{3,4},{4,3},{5,6},{6,5},{7,8},{8,7},{9,10},{10,9... | collective-permute-start | bytes 393224 | tf_op jit(solution)/shard_map/ppermute | solution.py:46
  173.4 22.0 %copy-start.8 = (f32[1024,256]{1,0:T(8,128)}, f32[1024,256]{1,0:T(8,128)S(1)}, u32[]{:S(2)}) copy-start(f32[1024,256]{1,0:T(8,128)S(1)} %get-tuple-element.64.r_ref) | copy-start | bytes 3145732
  173.4 3.6 %collective-permute-start.8 = (f32[128,256]{1,0:T(8,128)S(1)}, f32[128,256]{1,0:T(8,128)S(1)}, u32[]{:S(2)}, u32[]{:S(2)}) collective-permute-start(f32[128,256]{1,0:T(8,128)S(1)} %get-tuple-element.54), channel_id=1, source_target_pairs={{0,1},{1,0},{2,3},{3,2},{4,5},{5,4},{6,7},{7,6},{8,9},{9,8},{10,11... | collective-permute-start | bytes 393224 | tf_op jit(solution)/shard_map/ppermute | solution.py:46
  175.1 6.3 %collective-permute-start.9 = (f32[128,256]{1,0:T(8,128)S(1)}, f32[128,256]{1,0:T(8,128)S(1)}, u32[]{:S(2)}, u32[]{:S(2)}) collective-permute-start(f32[128,256]{1,0:T(8,128)S(1)} %get-tuple-element.55), channel_id=1, source_target_pairs={{0,0},{1,2},{2,1},{3,4},{4,3},{5,6},{6,5},{7,8},{8,7},{9,10},{10,9... | collective-permute-start | bytes 393224 | tf_op jit(solution)/shard_map/ppermute | solution.py:46
  210.7 32.5 %copy-start.9 = (f32[1024,256]{1,0:T(8,128)S(1)}, f32[1024,256]{1,0:T(8,128)}, u32[]{:S(2)}) copy-start(f32[1024,256]{1,0:T(8,128)} %copy-done.8) | copy-start | bytes 3145732
  215.4 1.0 copy-start.10
  216.3 1.0 copy-start.12
  217.3 0.7 copy-start.18
  218.0 0.7 copy-start.19
  218.6 24.6 %copy-start.7 = (f32[1024,256]{1,0:T(8,128)S(1)}, f32[1024,256]{1,0:T(8,128)}, u32[]{:S(2)}) copy-start(f32[1024,256]{1,0:T(8,128)} %copy-done.6) | copy-start | bytes 3145732
  219.5 22.9 %all-to-all-start.9 = ((f32[256,1,256]{2,1,0:T(1,128)}), f32[256,1,256]{2,1,0:T(1,128)S(1)}, u32[]{:S(2)}, u32[]{:S(2)}) async-start(f32[256,1,256]{2,1,0:T(1,128)} %broadcast_in_dim.63), calls=%async_computation.9 | async-start | bytes 524288 | tf_op jit(solution)/shard_map/all_to_all | solution.py:42
  226.1 17.1 %collective-permute-start.10 = (f32[128,256]{1,0:T(8,128)}, f32[128,256]{1,0:T(8,128)S(1)}, u32[]{:S(2)}, u32[]{:S(2)}) collective-permute-start(f32[128,256]{1,0:T(8,128)} %copy-done.19), channel_id=1, source_target_pairs={{0,1},{1,0},{2,3},{3,2},{4,5},{5,4},{6,7},{7,6},{8,9},{9,8},{10,11... | collective-permute-start | bytes 393224 | tf_op jit(solution)/shard_map/ppermute | solution.py:46
  228.5 14.8 %collective-permute-start.11 = (f32[128,256]{1,0:T(8,128)}, f32[128,256]{1,0:T(8,128)S(1)}, u32[]{:S(2)}, u32[]{:S(2)}) collective-permute-start(f32[128,256]{1,0:T(8,128)} %copy-done.18), channel_id=1, source_target_pairs={{0,0},{1,2},{2,1},{3,4},{4,3},{5,6},{6,5},{7,8},{8,7},{9,10},{10,9... | collective-permute-start | bytes 393224 | tf_op jit(solution)/shard_map/ppermute | solution.py:46
  243.3 1.2 copy-start.11
  244.5 1.2 copy-start.13
where the time goes:
time: 249 us; the launch traced here: 248 us
  blocking collectives  83.7 us (34%)
  starting transfers between devices  55 us (22%)
  local copies, waits for them, and re-layouts  34.1 us (14%)
  waiting for transfers between devices  31.1 us (12%)
  Pallas kernels  30 us (12%)
  other arithmetic  9.06 us (4%)
  matrix products  3.91 us (2%)
    all_to_all x6, blocking collectives, swap(): return lax.all_to_all(blocks, axis, split_axis=0, concat_axis=0, tiled=True)  83.7 us
    pallas_call x13, Pallas kernels, run(): pl.pallas_call(body, out_shape=[jax.ShapeDtypeStruct(s, F32) for s in out...  30 us
    all_to_all x4, starting transfers between devices, swap(): return lax.all_to_all(blocks, axis, split_axis=0, concat_axis=0, tiled=True)  29.5 us
    ppermute x12, starting transfers between devices, matched(): return lax.ppermute(value, CLUSTER_SUB, pairs)  25.6 us
    all_to_all x4, waiting for transfers between devices, swap(): return lax.all_to_all(blocks, axis, split_axis=0, concat_axis=0, tiled=True)  19.5 us
    ppermute x12, waiting for transfers between devices, matched(): return lax.ppermute(value, CLUSTER_SUB, pairs)  11.6 us
    unnamed x44, local copies, waits for them, and re-layouts  11 us
  transfers between devices with their start and end apart: 16, of which 5 were waited for; matrix products, arithmetic and copies ran while one was open for 13% of the time, Pallas kernels for 1%

commit v1 on v0

--- a/solution.py
+++ b/solution.py
@@ -15,13 +15,8 @@
 ROWS = 256
 VMEM_LIMIT = 24 * 1024 * 1024
 
-FULL = lax.Precision.HIGHEST
 F32 = jnp.float32
 BF16 = jnp.bfloat16
-
-
-def dot(a, b, precision=FULL):
-    return jnp.dot(a, b, precision=precision, preferred_element_type=F32)
 
 
 def fast(a, b):
@@ -31,11 +26,6 @@
 def halves(value):
     high = value.astype(BF16)
     return high, (value - high.astype(F32)).astype(BF16)
-
-
-def rounded_halves(value):
-    high = lax.reduce_precision(value, exponent_bits=8, mantissa_bits=7)
-    return high.astype(BF16), (value - high).astype(BF16)
 
 
 def swap(blocks, axis):
@@ -56,7 +46,7 @@
     def run(*operands):
         return pl.pallas_call(
             body,
-            out_shape=[jax.ShapeDtypeStruct(s, F32) for s in out_shapes],
+            out_shape=[s if hasattr(s, "dtype") else jax.ShapeDtypeStruct(s, F32) for s in out_shapes],
             in_specs=[pl.BlockSpec(memory_space=pltpu.VMEM)] * len(operands),
             out_specs=[pl.BlockSpec(memory_space=pltpu.VMEM)] * len(out_shapes),
             scratch_shapes=scratch,
@@ -77,7 +67,7 @@
 def stacked(amounts):
     spare = jnp.zeros((TILE, amounts.shape[1]), F32)
     high, low = halves(jnp.concatenate([amounts, spare], axis=0))
-    return jnp.concatenate([high, low, high], axis=0)
+    return jnp.concatenate([high, low, high, jnp.zeros_like(high)], axis=0)
 
 
 def blocks_of(rows, body, start):
@@ -191,17 +181,102 @@
     return sums + fast(rigid, zh), low_sums + fast(rigid, zl)
 
 
-def start_body(modes, y_ref, mate_ref, far_ref, st_ref, w_ref, rigid_ref, out_ref, pack_ref):
-    rh, rl = received(mate_ref, far_ref)
+def paired(value):
+    high, low = halves(value)
+    return jnp.concatenate([high.astype(F32), low.astype(F32)], axis=0).astype(BF16)
+
+
+def folded(pair):
+    return pair[:TILE] + pair[TILE:]
+
+
+def prepare_body(modes, group, gap_ref, coarse_ref, rigid_ref, s_ref, mate_ref, far_ref, wide_ref):
+    shared = s_ref.shape[1] // 2
+    cases = gap_ref.shape[1]
+
+    def step(at, i, sent):
+        high, rest = halves(gap_ref[at, :])
+        pick = s_ref[i]
+        low = rest.astype(F32)
+        tail = (gap_ref[at, :] - high.astype(F32) - low).astype(BF16)
+        return sent + (fast(pick, high) + fast(pick, rest) + fast(pick, tail))
+
+    sent = blocks_of(gap_ref.shape[0], step, jnp.zeros((2 * shared, cases), F32))
+    mate_ref[:shared, :] = sent[:shared]
+    far_ref[:shared, :] = sent[shared:]
+
+    narrow, wide = 4 * group * modes, 4 * group * TILE
+    column = lax.broadcasted_iota(jnp.int32, (narrow, wide), 1)
+    source = (column // TILE) * modes + column % TILE
+    source = jnp.where(column % TILE < modes, source, -1)
+    widen = jnp.where(lax.broadcasted_iota(jnp.int32, (narrow, wide), 0) == source, 1.0, 0.0).astype(BF16)
+    for part in range(coarse_ref.shape[1] // narrow):
+        spread = folded(fast(paired(coarse_ref[:, part * narrow:(part + 1) * narrow]), widen))
+        for piece in range(wide // cases):
+            top = shared + TILE * (part * (wide // cases) + piece)
+            value = spread[:, piece * cases:(piece + 1) * cases]
+            mate_ref[top:top + TILE, :] = value
+            far_ref[top:top + TILE, :] = value
+
+    picked = jnp.zeros((2 * TILE, 2 * shared), F32)
+    for i in range(s_ref.shape[0]):
+        rigid = paired(rigid_ref[:, i * ROWS:(i + 1) * ROWS])
+        wide_ref[i] = rigid
+        picked = picked + lax.dot_general(
+            rigid, s_ref[i], (((1,), (1,)), ((), ())), preferred_element_type=F32
+        )
+    picked = folded(picked)
+    spare = jnp.zeros((TILE, cases - shared), F32)
+    last = mate_ref.shape[0] - TILE
+    mate_ref[last:, :] = jnp.concatenate([picked[:, :shared], spare], axis=1)
+    far_ref[last:, :] = jnp.concatenate([picked[:, shared:], spare], axis=1)
+
+
+def tile_body(modes, shared, own_ref, mate_ref, far_ref, out_ref):
+    wide = out_ref.shape[2]
+    row = lax.broadcasted_iota(jnp.int32, (TILE, wide), 0)
+    column = lax.broadcasted_iota(jnp.int32, (TILE, wide), 1)
+    ones = jnp.where((row >= modes) & (column % TILE == row), 1.0, 0.0)
+    per_row = own_ref.shape[1] // wide
+    for member in range(out_ref.shape[0]):
+        top = shared + TILE * (member // per_row)
+        left = wide * (member % per_row)
+        at = (slice(top, top + TILE), slice(left, left + wide))
+        out_ref[member, :TILE, :] = own_ref[at] + ones
+        out_ref[member, TILE:2 * TILE, :] = mate_ref[at]
+        out_ref[member, 2 * TILE:, :] = far_ref[at]
+
+
+def start_body(modes, y_ref, mate_ref, far_ref, st_ref, w_ref, wide_ref, out_ref, pack_ref, tall_ref):
+    shared = st_ref.shape[1] // 2
     cases = y_ref.shape[1]
+    rows = jnp.concatenate([mate_ref[:shared, :], far_ref[:shared, :]], axis=0)
+    rh, rest = halves(rows)
+    rt = (rows - rh.astype(F32) - rest.astype(F32)).astype(BF16)
+    last = mate_ref.shape[0] - TILE
+    near_mate = paired(mate_ref[last:, :shared])
+    near_far = paired(far_ref[last:, :shared])
+    spare = jnp.zeros((TILE, ROWS), F32)
 
     def step(at, i, carry):
         size, sums, low_sums = carry
         place = st_ref[at, :]
-        value = y_ref[at, :] + (fast(place, rh) + fast(place, rl))
+        value = y_ref[at, :] + (fast(place, rh) + fast(place, rest) + fast(place, rt))
         out_ref[at, :] = value
         size = size + jnp.sum(w_ref[at, :] * value * value, axis=0, keepdims=True)
-        return (size, *gather_modes(rigid_ref, value, i, sums, low_sums))
+
+        def across(near, hot):
+            return folded(lax.dot_general(near, hot, (((1,), (1,)), ((), ())), preferred_element_type=F32))
+
+        own = folded(wide_ref[i].astype(F32))
+        stack = jnp.concatenate(
+            [own, across(near_mate, place[:, :shared]), across(near_far, place[:, shared:]), spare], axis=0
+        )
+        high, low = halves(stack)
+        high, low = high.astype(F32), low.astype(F32)
+        stack = jnp.concatenate([high, high, low, jnp.zeros_like(low)], axis=0)
+        tall_ref[at, :] = stack.T.astype(BF16)
+        return (size, *gather_modes(wide_ref, value, i, sums, low_sums))
 
     zeros = jnp.zeros((2 * TILE, cases), F32)
     size, sums, low_sums = blocks_of(y_ref.shape[0], step, (jnp.zeros((1, cases), F32), zeros, zeros))
@@ -232,7 +307,10 @@
 def block_body(block_ref, near_ref, out_ref):
     members, tile, cases = near_ref.shape
     high, low = halves(near_ref[...].reshape(members * tile, cases))
-    out = fast(block_ref[...], jnp.concatenate([high, low, high], axis=0))
+    outer, tall, wide = block_ref.shape
+    block_high, block_low = halves(block_ref[...].reshape(outer * tall, wide))
+    block = jnp.concatenate([block_high, block_high, block_low], axis=1)
+    out = fast(block, jnp.concatenate([high, low, high], axis=0))
     out_ref[...] = out.reshape(out_ref.shape)
 
 
@@ -269,66 +347,16 @@
         from_mate = matched(to_mate, mate_pairs)
         return from_mate, from_far
 
-    gap_near = exchanged(gap_raw[mate], gap_raw[far])
-
     picks = jnp.concatenate([mate, far])
     live = jnp.concatenate([jnp.ones((shared,), F32), jnp.full((shared,), inside)])
-    one_hot = jnp.where(
-        picks[:, None] == lax.broadcasted_iota(jnp.int32, (2 * shared, local_rows), 1), live[:, None], 0.0
-    )
-    selector = one_hot.astype(BF16).reshape(2 * shared, local_rows // ROWS, ROWS).transpose(1, 0, 2)
+    blocks = (local_rows // ROWS, 2 * shared, ROWS)
+    numbers = lax.broadcasted_iota(jnp.int32, blocks, 0) * ROWS + lax.broadcasted_iota(jnp.int32, blocks, 2)
+    selector = jnp.where(picks[None, :, None] == numbers, live[None, :, None], 0.0).astype(BF16)
     placer = jnp.where(
         picks[None, :] == lax.broadcasted_iota(jnp.int32, (local_rows, 2 * shared), 0), live[None, :], 0.0
     )
     weights = jnp.broadcast_to(1.0 - 0.5 * jnp.sum(placer, axis=1, keepdims=True), (local_rows, cases))
     placer = placer.astype(BF16)
-
-    rigid_shared = lax.dot_general(
-        rigid_images, one_hot, (((1,), (1,)), ((), ())), precision=FULL, preferred_element_type=F32
-    )
-    from_mate, from_far = exchanged(
-        jnp.concatenate([coarse_rows, rigid_shared[:, :shared]], axis=1),
-        jnp.concatenate([coarse_rows, rigid_shared[:, shared:]], axis=1),
-    )
-    order = coarse_rows.shape[1]
-
-    def across(near, hot):
-        return lax.dot_general(
-            hot, near, (((0,), (1,)), ((), ())), precision=FULL, preferred_element_type=F32
-        )
-
-    gap = jnp.zeros((local_rows, TILE - modes), F32)
-    rigid_tall = jnp.concatenate(
-        [
-            rigid_images.T,
-            gap,
-            across(from_mate[:, order:], one_hot[:shared]),
-            gap,
-            across(from_far[:, order:], one_hot[shared:]),
-            gap,
-            jnp.zeros((local_rows, TILE), F32),
-        ],
-        axis=1,
-    )
-    tall_high, tall_low = rounded_halves(rigid_tall)
-    rigid_tall = jnp.concatenate([tall_high, tall_high, tall_low], axis=1)
-    wide_high, wide_low = rounded_halves(jnp.pad(rigid_images, ((0, TILE - modes), (0, 0))))
-    rigid_wide = jnp.concatenate([wide_high, wide_low], axis=0)
-    rigid_wide = rigid_wide.reshape(2 * TILE, local_rows // ROWS, ROWS).transpose(1, 0, 2)
-
-    rows_here = jnp.concatenate([coarse_rows, from_mate[:, :order], from_far[:, :order]], axis=0)
-    block = swap(rows_here.reshape(3 * modes, outer, inner * modes).transpose(1, 0, 2), OUTER)
-    block = jnp.pad(
-        block.reshape(outer, 3, modes, inner, modes),
-        ((0, 0), (0, 0), (0, TILE - modes), (0, 0), (0, TILE - modes)),
-    )
-    shape = (1, 3, TILE, 1, TILE)
-    part_of = lax.broadcasted_iota(jnp.int32, shape, 1)
-    tile_row = lax.broadcasted_iota(jnp.int32, shape, 2)
-    tile_col = lax.broadcasted_iota(jnp.int32, shape, 4)
-    sums = ((part_of == 0) & (tile_row == tile_col) & (tile_row >= modes)).astype(F32)
-    block_high, block_low = rounded_halves((block + sums).reshape(outer * 3 * TILE, inner * TILE))
-    block = jnp.concatenate([block_high, block_high, block_low], axis=1)
 
     field = (local_rows, cases)
     edge = (shared, cases)
@@ -341,9 +369,28 @@
     light = 4 * local_rows * cases * 2 * shared
     moved = 4 * local_rows * (local_rows + 3 * cases)
 
+    def shaped(shape, dtype):
+        return jax.ShapeDtypeStruct(shape, dtype)
+
+    pad = ((0, TILE - modes), (0, 0))
+    payload = (shared + TILE * (outer * inner * TILE // cases) + TILE, cases)
+    to_mate, to_far, rigid_wide = call(
+        functools.partial(prepare_body, modes, inner),
+        [payload, payload, shaped((local_rows // ROWS, 2 * TILE, ROWS), BF16)], [], light, 8 * local_rows * cases,
+    )(gap_raw, jnp.pad(coarse_rows, pad), jnp.pad(rigid_images, pad), selector)
+    from_mate, from_far = exchanged(to_mate, to_far)
+    from_mate, from_far, placer, weights = lax.optimization_barrier((from_mate, from_far, placer, weights))
+    [block] = call(
+        functools.partial(tile_body, modes, shared), [(outer, 3 * TILE, inner * TILE)], [], 1, 8 * local_rows
+    )(to_mate, from_mate, from_far)
+    block = swap(block, OUTER)
+    block, from_mate, from_far, placer, weights = lax.optimization_barrier(
+        (block, from_mate, from_far, placer, weights)
+    )
+
     def coarse(pack):
         near = swap(pack, INNER)
-        [rows] = call(block_body, [(outer, 3 * TILE, cases)], [], 6 * block.shape[0] * block.shape[1] * cases,
+        [rows] = call(block_body, [(outer, 3 * TILE, cases)], [], 6 * outer * 3 * TILE * inner * TILE * cases,
                       4 * outer * 4 * TILE * cases)(block, near)
         return swap(rows, OUTER)
 
@@ -351,9 +398,10 @@
         body = functools.partial(assemble_body, modes, weighted, sized)
         return call(body, [field, pack_shape], [], light, 12 * local_rows * cases)(*operands)
 
-    residual, pack = call(functools.partial(start_body, modes), [field, pack_shape], [], light, 12 * local_rows * cases)(
-        gap_raw, *gap_near, placer, weights, rigid_wide
-    )
+    residual, pack, rigid_tall = call(
+        functools.partial(start_body, modes), [field, pack_shape, shaped((local_rows, 128), BF16)], [], light,
+        12 * local_rows * cases,
+    )(gap_raw, from_mate, from_far, placer, weights, rigid_wide)
     near = coarse(pack)
     out, to_mate, to_far, part, amounts = call(
         precondition_first, [field, edge, edge, row, rows_out], scratch, big, moved
@@ -374,14 +422,15 @@
     out, to_mate, to_far, part, last, direction = call(
         functools.partial(direct_next, modes), [field, edge, edge, row, rows_out, field], own, big, moved
     )(near, total, smoothed, direction_first, rigid_tall, dual_ops, selector)
-    norm_second = last[modes + 1]
+    norms = jnp.stack([norm_first, last[modes + 1]])
     from_mate, from_far = exchanged(to_mate, to_far)
+    part, from_mate, from_far, norms = lax.optimization_barrier((part, from_mate, from_far, norms))
     bending = jnp.sum(swap(jnp.broadcast_to(part, (count, 1, cases)), CLUSTER_SUB), axis=0)
     step = last[modes:modes + 1] / bending
     multipliers, residual = call(finish_body, [field, field], [], light, 24 * local_rows * cases)(
         out, from_mate, from_far, placer, residual, direction_first, direction, step_first, step
     )
-    return (multipliers, residual, jnp.stack([norm_first, norm_second]))
+    return (multipliers, residual, norms)
 
 
 def solution(mesh):

time: 249 us -> 233 us (0.936)
  blocking collectives: 83.7 us -> 150 us
  starting transfers between devices: 55 us -> 20.1 us
  local copies, waits for them, and re-layouts: 34.1 us -> 7.53 us
  waiting for transfers between devices: 31.1 us -> 21 us
  other arithmetic: 9.06 us -> 2.22 us
  matrix products: 3.91 us -> 0 us
    all_to_all x6 -> x10, blocking collectives: 83.7 us -> 150 us  [swap(): return lax.all_to_all(blocks, axis, split_axis=0, concat_axis=0, tiled=True)]
    all_to_all x4 -> x0, starting transfers between devices: 29.5 us -> none  [swap(): return lax.all_to_all(blocks, axis, split_axis=0, concat_axis=0, tiled=True)]
    all_to_all x4 -> x0, waiting for transfers between devices: 19.5 us -> none  [swap(): return lax.all_to_all(blocks, axis, split_axis=0, concat_axis=0, tiled=True)]
    ppermute x12 -> x10, waiting for transfers between devices: 11.6 us -> 21 us  [matched(): return lax.ppermute(value, CLUSTER_SUB, pairs)]
    reshape x4 -> x0, local copies, waits for them, and re-layouts: 7.06 us -> none  [the longest x1 3.05 us: shards(): (block + sums).reshape(outer * 3 * TILE, inner * TILE)]
    ppermute x12 -> x10, starting transfers between devices: 25.6 us -> 20.1 us  [matched(): return lax.ppermute(value, CLUSTER_SUB, pairs)]
    unnamed x44 -> x16, local copies, waits for them, and re-layouts: 11 us -> 5.61 us
    add x1 -> x0, local copies, waits for them, and re-layouts: 4.62 us -> none  [shards(): block + sums]
  transfers between devices with their start and end apart: 16 -> 10, of which waited for: 5 -> 5; matrix products, arithmetic and copies ran while one was open for 13% -> 0% of each run, Pallas kernels for 1% -> 0%
where the time goes in v1:
time: 233 us; the launch traced here: 232 us
  blocking collectives  150 us (64%)
  Pallas kernels  31.1 us (13%)
  waiting for transfers between devices  21 us (9%)
  starting transfers between devices  20.1 us (9%)
  local copies, waits for them, and re-layouts  7.53 us (3%)
    all_to_all x10, blocking collectives, swap(): return lax.all_to_all(blocks, axis, split_axis=0, concat_axis=0, tiled=True)  150 us
    pallas_call x15, Pallas kernels, run(): pl.pallas_call(body, out_shape=[s if hasattr(s, 'dtype') else jax.ShapeDt...  31.1 us
    ppermute x10, waiting for transfers between devices, matched(): return lax.ppermute(value, CLUSTER_SUB, pairs)  21 us
    ppermute x10, starting transfers between devices, matched(): return lax.ppermute(value, CLUSTER_SUB, pairs)  20.1 us
    unnamed x16, local copies, waits for them, and re-layouts  5.61 us
  transfers between devices with their start and end apart: 10, of which 5 were waited for; matrix products, arithmetic and copies ran while one was open for 0% of the time, Pallas kernels for 0%

profile of v1, /device:TPU:1, one launch (start us, length us, event | category | flops | bytes accessed | tf_op | source)
XLA Modules:
  0.0 232.5 jit_solution(2912248892909666467)
XLA Ops:
  0.7 0.8 pad.9.coarse_ref
  1.5 0.8 pad.10.rigid_ref
  2.2 0.8 fusion
  3.0 0.2 select_convert_fusion.1.s_ref
  3.2 0.0 copy-start.2
  3.2 1.2 copy-done.2
  4.4 1.6 shard_map.85
  6.1 3.2 %collective-permute-start = (f32[200,256]{1,0:T(8,128)S(1)}, f32[200,256]{1,0:T(8,128)S(1)}, u32[]{:S(2)}, u32[]{:S(2)}) collective-permute-start(f32[200,256]{1,0:T(8,128)S(1)} %get-tuple-element.54.own_ref), channel_id=1, source_target_pairs={{0,1},{1,0},{2,3},{3,2},{4,5},{5,4},{6,7},{7,6},{8,9},{9,8},{10,11... | collective-permute-start | bytes 614408 | tf_op jit(solution)/shard_map/ppermute | solution.py:36
  9.3 2.0 collective-permute-start.1
  11.3 0.2 select_reduce_fusion
  11.5 0.2 select_convert_fusion.st_ref.refs_3_
  11.7 0.0 collective-permute-done.mate_ref
  11.7 4.6 %collective-permute-done.1.far_ref = f32[200,256]{1,0:T(8,128)S(1)} collective-permute-done((f32[200,256]{1,0:T(8,128)S(1)}, f32[200,256]{1,0:T(8,128)S(1)}, u32[]{:S(2)}, u32[]{:S(2)}) %collective-permute-start.1) | collective-permute-done | bytes 204832 | tf_op jit(solution)/shard_map/ppermute | solution.py:36
  16.4 0.2 broadcast_in_dim.46.w_ref.refs_6_
  16.6 11.9 %all_to_all.50.block_ref = f32[16,24,128]{2,1,0:T(8,128)S(1)} all-to-all(f32[16,24,128]{2,1,0:T(8,128)S(1)} %shard_map.86), channel_id=1, replica_groups=mesh['cluster'=4,'sub_0'=4,'sub_1'=8,'sub_2'=2] {'cluster','sub_0'}, dimensions={0} | all-to-all | bytes 393216 | tf_op jit(solution)/shard_map/all_to_all | solution.py:32
  28.5 0.0 copy-done.3
  28.5 2.1 shard_map.87
  30.6 20.0 %all_to_all.51.near_ref = f32[16,8,256]{2,1,0:T(8,128)S(1)} all-to-all(f32[16,8,256]{2,1,0:T(8,128)S(1)} %get-tuple-element.66), channel_id=1, replica_groups=mesh['cluster'=4,'sub_0'=4,'sub_1'=8,'sub_2'=2] {'sub_1','sub_2'}, dimensions={0} | all-to-all | bytes 262144 | tf_op jit(solution)/shard_map/all_to_all | solution.py:32
  50.7 0.3 shard_map.88
  50.9 12.2 %all_to_all.52.near_ref = f32[16,24,256]{2,1,0:T(8,128)S(1)} all-to-all(f32[16,24,256]{2,1,0:T(8,128)S(1)} %shard_map.88), channel_id=1, replica_groups=mesh['cluster'=4,'sub_0'=4,'sub_1'=8,'sub_2'=2] {'cluster','sub_0'}, dimensions={0} | all-to-all | bytes 786432 | tf_op jit(solution)/shard_map/all_to_all | solution.py:32
  63.1 0.0 copy-done
  63.1 4.7 %shard_map.89 = (f32[1024,256]{1,0:T(8,128)S(1)}, f32[128,256]{1,0:T(8,128)S(1)}, f32[128,256]{1,0:T(8,128)S(1)}, f32[1,256]{1,0:T(1,128)S(1)}, f32[24,256]{1,0:T(8,128)S(1)}) custom-call(f32[16,24,256]{2,1,0:T(8,128)S(1)} %all_to_all.52.near_ref, f32[1024,256]{1,0:T(8,128)S(1)} %get-tuple-element.67.r_ref, f32[1024,256]{1,0:T(8,128)S(1)} %broadcast_in_dim.46.w_ref.refs_6_, ...), custom_call_target="tpu_custom_call" | custom-call | flops 1610612736 | bytes 7340032 | tf_op jit(solution)/shard_map/pallas_call | solution.py:47
  67.8 0.0 copy-start.1
  67.8 1.8 collective-permute-start.2
  69.6 2.4 %collective-permute-start.3 = (f32[128,256]{1,0:T(8,128)S(1)}, f32[128,256]{1,0:T(8,128)S(1)}, u32[]{:S(2)}, u32[]{:S(2)}) collective-permute-start(f32[128,256]{1,0:T(8,128)S(1)} %get-tuple-element.71), channel_id=1, source_target_pairs={{0,0},{1,2},{2,1},{3,4},{4,3},{5,6},{6,5},{7,8},{8,7},{9,10},{10,9... | collective-permute-start | bytes 393224 | tf_op jit(solution)/shard_map/ppermute | solution.py:36
  72.0 0.0 collective-permute-done.2.refs_1_
  72.0 3.9 %collective-permute-done.3.refs_2_ = f32[128,256]{1,0:T(8,128)S(1)} collective-permute-done((f32[128,256]{1,0:T(8,128)S(1)}, f32[128,256]{1,0:T(8,128)S(1)}, u32[]{:S(2)}, u32[]{:S(2)}) %collective-permute-start.3) | collective-permute-done | bytes 131104 | tf_op jit(solution)/shard_map/ppermute | solution.py:36
  75.9 1.8 shard_map.90
  77.7 12.7 %all_to_all.53.near_ref = f32[16,8,256]{2,1,0:T(8,128)S(1)} all-to-all(f32[16,8,256]{2,1,0:T(8,128)S(1)} %get-tuple-element.73), channel_id=1, replica_groups=mesh['cluster'=4,'sub_0'=4,'sub_1'=8,'sub_2'=2] {'sub_1','sub_2'}, dimensions={0} | all-to-all | bytes 262144 | tf_op jit(solution)/shard_map/all_to_all | solution.py:32
  90.4 0.3 shard_map.91
  90.6 15.0 %all_to_all.54.near_ref = f32[16,24,256]{2,1,0:T(8,128)S(1)} all-to-all(f32[16,24,256]{2,1,0:T(8,128)S(1)} %shard_map.91), channel_id=1, replica_groups=mesh['cluster'=4,'sub_0'=4,'sub_1'=8,'sub_2'=2] {'cluster','sub_0'}, dimensions={0} | all-to-all | bytes 786432 | tf_op jit(solution)/shard_map/all_to_all | solution.py:32
  105.7 4.6 %shard_map.92 = (f32[1024,256]{1,0:T(8,128)S(1)}, f32[128,256]{1,0:T(8,128)S(1)}, f32[128,256]{1,0:T(8,128)S(1)}, f32[1,256]{1,0:T(1,128)S(1)}, f32[24,256]{1,0:T(8,128)S(1)}, /*index=5*/f32[1024,256]{1,0:T(8,128)S(1)}) custom-call(f32[16,24,256]{2,1,0:T(8,128)S(1)} %all_to_all.54.near_ref, f32[1024,256]{1,0:T(8,128)S(1)} %get-tuple-element.74.v_ref, ...), custom_call_target="tpu_custom_call" | custom-call | flops 1610612736 | bytes 7340032 | tf_op jit(solution)/shard_map/pallas_call | solution.py:47
  110.3 1.7 collective-permute-start.4
  112.0 1.9 collective-permute-start.5
  113.9 0.0 collective-permute-done.4.refs_1_
  113.9 4.3 %collective-permute-done.5.refs_2_ = f32[128,256]{1,0:T(8,128)S(1)} collective-permute-done((f32[128,256]{1,0:T(8,128)S(1)}, f32[128,256]{1,0:T(8,128)S(1)}, u32[]{:S(2)}, u32[]{:S(2)}) %collective-permute-start.5) | collective-permute-done | bytes 131104 | tf_op jit(solution)/shard_map/ppermute | solution.py:36
  118.3 1.8 shard_map.93
  120.0 12.2 %all_to_all.55.near_ref = f32[16,8,256]{2,1,0:T(8,128)S(1)} all-to-all(f32[16,8,256]{2,1,0:T(8,128)S(1)} %get-tuple-element.79), channel_id=1, replica_groups=mesh['cluster'=4,'sub_0'=4,'sub_1'=8,'sub_2'=2] {'sub_1','sub_2'}, dimensions={0} | all-to-all | bytes 262144 | tf_op jit(solution)/shard_map/all_to_all | solution.py:32
  132.2 0.3 shard_map.94
  132.5 15.1 %all_to_all.56.near_ref = f32[16,24,256]{2,1,0:T(8,128)S(1)} all-to-all(f32[16,24,256]{2,1,0:T(8,128)S(1)} %shard_map.94), channel_id=1, replica_groups=mesh['cluster'=4,'sub_0'=4,'sub_1'=8,'sub_2'=2] {'cluster','sub_0'}, dimensions={0} | all-to-all | bytes 786432 | tf_op jit(solution)/shard_map/all_to_all | solution.py:32
  147.5 4.7 %shard_map.95 = (f32[1024,256]{1,0:T(8,128)S(1)}, f32[128,256]{1,0:T(8,128)S(1)}, f32[128,256]{1,0:T(8,128)S(1)}, f32[1,256]{1,0:T(1,128)S(1)}, f32[1,256]{1,0:T...) custom-call(f32[16,24,256]{2,1,0:T(8,128)S(1)} %all_to_all.56.near_ref, ...), custom_call_target="tpu_custom_call" | custom-call | flops 1610612736 | bytes 7340032 | tf_op jit(solution)/shard_map/pallas_call | solution.py:47
  152.2 1.7 collective-permute-start.6
  153.9 1.9 collective-permute-start.7
  155.9 0.0 collective-permute-done.6.refs_1_
  155.9 4.3 %collective-permute-done.7.refs_2_ = f32[128,256]{1,0:T(8,128)S(1)} collective-permute-done((f32[128,256]{1,0:T(8,128)S(1)}, f32[128,256]{1,0:T(8,128)S(1)}, u32[]{:S(2)}, u32[]{:S(2)}) %collective-permute-start.7) | collective-permute-done | bytes 131104 | tf_op jit(solution)/shard_map/ppermute | solution.py:36
  160.2 1.8 shard_map.96
  162.0 12.2 %all_to_all.57.near_ref = f32[16,8,256]{2,1,0:T(8,128)S(1)} all-to-all(f32[16,8,256]{2,1,0:T(8,128)S(1)} %get-tuple-element.88), channel_id=1, replica_groups=mesh['cluster'=4,'sub_0'=4,'sub_1'=8,'sub_2'=2] {'sub_1','sub_2'}, dimensions={0} | all-to-all | bytes 262144 | tf_op jit(solution)/shard_map/all_to_all | solution.py:32
  174.2 0.3 shard_map.97
  174.5 15.0 %all_to_all.58.near_ref = f32[16,24,256]{2,1,0:T(8,128)S(1)} all-to-all(f32[16,24,256]{2,1,0:T(8,128)S(1)} %shard_map.97), channel_id=1, replica_groups=mesh['cluster'=4,'sub_0'=4,'sub_1'=8,'sub_2'=2] {'cluster','sub_0'}, dimensions={0} | all-to-all | bytes 786432 | tf_op jit(solution)/shard_map/all_to_all | solution.py:32
  189.5 4.7 %shard_map.98 = (f32[1024,256]{1,0:T(8,128)S(1)}, f32[128,256]{1,0:T(8,128)S(1)}, f32[128,256]{1,0:T(8,128)S(1)}, f32[1,256]{1,0:T(1,128)S(1)}, f32[24,256]{1,0:T(8,128)S(1)}, /*index=5*/f32[1024,256]{1,0:T(8,128)S(1)}) custom-call(f32[16,24,256]{2,1,0:T(8,128)S(1)} %all_to_all.58.near_ref, f32[24,256]{1,0:T(8,128)S(1)} %get-tuple-element.81.norm_ref, ...), custom_call_target="tpu_custom_call" | custom-call | flops 1610612736 | bytes 7340032 | tf_op jit(solution)/shard_map/pallas_call | solution.py:47
  194.2 0.0 copy-start.4
  194.2 1.0 copy-done.4
  195.1 1.0 copy-done.6
  196.1 1.6 collective-permute-start.8
  197.7 1.9 collective-permute-start.9
  199.7 0.6 pad_maximum_fusion
  200.3 0.0 collective-permute-done.8.mate_ref
  200.3 3.7 %collective-permute-done.9.far_ref = f32[128,256]{1,0:T(8,128)S(1)} collective-permute-done((f32[128,256]{1,0:T(8,128)S(1)}, f32[128,256]{1,0:T(8,128)S(1)}, u32[]{:S(2)}, u32[]{:S(2)}) %collective-permute-start.9) | collective-permute-done | bytes 131104 | tf_op jit(solution)/shard_map/ppermute | solution.py:36
  204.0 0.1 broadcast_in_dim.47
  204.2 23.2 %all_to_all.59 = f32[256,1,256]{2,1,0:T(1,128)S(1)} all-to-all(f32[256,1,256]{2,1,0:T(1,128)S(1)} %broadcast_in_dim.47), channel_id=1, replica_groups=mesh['cluster'=4,'sub_0'=4,'sub_1'=8,'sub_2'=2] {'cluster','sub_0','sub_..., dimensions={0} | all-to-all | bytes 524288 | tf_op jit(solution)/shard_map/all_to_all | solution.py:32
  227.4 0.3 reduce_sum.21
  227.7 1.2 copy-done.5
  228.9 1.2 copy-done.7
  230.2 2.3 shard_map.99
  (15 shorter events, 0.1 us)
Async XLA Ops:
  3.2 1.2 copy-start.2
  4.4 24.1 %copy-start.3 = (f32[1024,256]{1,0:T(8,128)S(1)}, f32[1024,256]{1,0:T(8,128)}, u32[]{:S(2)}) copy-start(f32[1024,256]{1,0:T(8,128)} %y_ref.1) | copy-start | bytes 3145732
  6.1 57.0 %copy-start = (f32[1024,1024]{1,0:T(8,128)S(1)}, f32[1024,1024]{1,0:T(8,128)}, u32[]{:S(2)}) copy-start(f32[1024,1024]{1,0:T(8,128)} %m_ref.6) | copy-start | bytes 12582916
  6.1 5.6 %collective-permute-start = (f32[200,256]{1,0:T(8,128)S(1)}, f32[200,256]{1,0:T(8,128)S(1)}, u32[]{:S(2)}, u32[]{:S(2)}) collective-permute-start(f32[200,256]{1,0:T(8,128)S(1)} %get-tuple-element.54.own_ref), channel_id=1, source_target_pairs={{0,1},{1,0},{2,3},{3,2},{4,5},{5,4},{6,7},{7,6},{8,9},{9,8},{10,11... | collective-permute-start | bytes 614408 | tf_op jit(solution)/shard_map/ppermute | solution.py:36
  9.3 7.1 %collective-permute-start.1 = (f32[200,256]{1,0:T(8,128)S(1)}, f32[200,256]{1,0:T(8,128)S(1)}, u32[]{:S(2)}, u32[]{:S(2)}) collective-permute-start(f32[200,256]{1,0:T(8,128)S(1)} %get-tuple-element.55), channel_id=1, source_target_pairs={{0,0},{1,2},{2,1},{3,4},{4,3},{5,6},{6,5},{7,8},{8,7},{9,10},{10,9... | collective-permute-start | bytes 614408 | tf_op jit(solution)/shard_map/ppermute | solution.py:36
  67.8 37.9 %copy-start.1 = (f32[1024,1024]{1,0:T(8,128)S(1)}, f32[1024,1024]{1,0:T(8,128)}, u32[]{:S(2)}) copy-start(f32[1024,1024]{1,0:T(8,128)} %m_ref.7) | copy-start | bytes 12582916
  67.8 4.2 %collective-permute-start.2 = (f32[128,256]{1,0:T(8,128)S(1)}, f32[128,256]{1,0:T(8,128)S(1)}, u32[]{:S(2)}, u32[]{:S(2)}) collective-permute-start(f32[128,256]{1,0:T(8,128)S(1)} %get-tuple-element.70), channel_id=1, source_target_pairs={{0,1},{1,0},{2,3},{3,2},{4,5},{5,4},{6,7},{7,6},{8,9},{9,8},{10,11... | collective-permute-start | bytes 393224 | tf_op jit(solution)/shard_map/ppermute | solution.py:36
  69.6 6.3 %collective-permute-start.3 = (f32[128,256]{1,0:T(8,128)S(1)}, f32[128,256]{1,0:T(8,128)S(1)}, u32[]{:S(2)}, u32[]{:S(2)}) collective-permute-start(f32[128,256]{1,0:T(8,128)S(1)} %get-tuple-element.71), channel_id=1, source_target_pairs={{0,0},{1,2},{2,1},{3,4},{4,3},{5,6},{6,5},{7,8},{8,7},{9,10},{10,9... | collective-permute-start | bytes 393224 | tf_op jit(solution)/shard_map/ppermute | solution.py:36
  110.3 3.6 %collective-permute-start.4 = (f32[128,256]{1,0:T(8,128)S(1)}, f32[128,256]{1,0:T(8,128)S(1)}, u32[]{:S(2)}, u32[]{:S(2)}) collective-permute-start(f32[128,256]{1,0:T(8,128)S(1)} %get-tuple-element.76), channel_id=1, source_target_pairs={{0,1},{1,0},{2,3},{3,2},{4,5},{5,4},{6,7},{7,6},{8,9},{9,8},{10,11... | collective-permute-start | bytes 393224 | tf_op jit(solution)/shard_map/ppermute | solution.py:36
  112.0 6.3 %collective-permute-start.5 = (f32[128,256]{1,0:T(8,128)S(1)}, f32[128,256]{1,0:T(8,128)S(1)}, u32[]{:S(2)}, u32[]{:S(2)}) collective-permute-start(f32[128,256]{1,0:T(8,128)S(1)} %get-tuple-element.77), channel_id=1, source_target_pairs={{0,0},{1,2},{2,1},{3,4},{4,3},{5,6},{6,5},{7,8},{8,7},{9,10},{10,9... | collective-permute-start | bytes 393224 | tf_op jit(solution)/shard_map/ppermute | solution.py:36
  152.2 3.6 %collective-permute-start.6 = (f32[128,256]{1,0:T(8,128)S(1)}, f32[128,256]{1,0:T(8,128)S(1)}, u32[]{:S(2)}, u32[]{:S(2)}) collective-permute-start(f32[128,256]{1,0:T(8,128)S(1)} %get-tuple-element.84), channel_id=1, source_target_pairs={{0,1},{1,0},{2,3},{3,2},{4,5},{5,4},{6,7},{7,6},{8,9},{9,8},{10,11... | collective-permute-start | bytes 393224 | tf_op jit(solution)/shard_map/ppermute | solution.py:36
  153.9 6.3 %collective-permute-start.7 = (f32[128,256]{1,0:T(8,128)S(1)}, f32[128,256]{1,0:T(8,128)S(1)}, u32[]{:S(2)}, u32[]{:S(2)}) collective-permute-start(f32[128,256]{1,0:T(8,128)S(1)} %get-tuple-element.85), channel_id=1, source_target_pairs={{0,0},{1,2},{2,1},{3,4},{4,3},{5,6},{6,5},{7,8},{8,7},{9,10},{10,9... | collective-permute-start | bytes 393224 | tf_op jit(solution)/shard_map/ppermute | solution.py:36
  194.2 1.0 copy-start.4
  195.1 1.0 copy-start.6
  196.1 4.2 %collective-permute-start.8 = (f32[128,256]{1,0:T(8,128)S(1)}, f32[128,256]{1,0:T(8,128)S(1)}, u32[]{:S(2)}, u32[]{:S(2)}) collective-permute-start(f32[128,256]{1,0:T(8,128)S(1)} %get-tuple-element.93), channel_id=1, source_target_pairs={{0,1},{1,0},{2,3},{3,2},{4,5},{5,4},{6,7},{7,6},{8,9},{9,8},{10,11... | collective-permute-start | bytes 393224 | tf_op jit(solution)/shard_map/ppermute | solution.py:36
  197.7 6.3 %collective-permute-start.9 = (f32[128,256]{1,0:T(8,128)S(1)}, f32[128,256]{1,0:T(8,128)S(1)}, u32[]{:S(2)}, u32[]{:S(2)}) collective-permute-start(f32[128,256]{1,0:T(8,128)S(1)} %get-tuple-element.94), channel_id=1, source_target_pairs={{0,0},{1,2},{2,1},{3,4},{4,3},{5,6},{6,5},{7,8},{8,7},{9,10},{10,9... | collective-permute-start | bytes 393224 | tf_op jit(solution)/shard_map/ppermute | solution.py:36
  227.7 1.2 copy-start.5
  228.9 1.2 copy-start.7

commit v2 on v1

--- a/solution.py
+++ b/solution.py
@@ -38,7 +38,7 @@
 
 def matchings(count):
     near = [(i, i ^ 1) for i in range(count)]
-    far = [(i, i if i in (0, count - 1) else ((i + 1) ^ 1) - 1) for i in range(count)]
+    far = [(i, (((i + 1) ^ 1) - 1) % count) for i in range(count)]
     return near, far
 
 
@@ -74,63 +74,91 @@
     return lax.fori_loop(0, rows // ROWS, lambda i, c: body(pl.ds(pl.multiple_of(i * ROWS, ROWS), ROWS), i, c), start)
 
 
-def multiply(m_ref, s_ref, x_ref, high_ref, low_ref, out_ref, mate_ref, far_ref, part_ref):
-    rows, cases = out_ref.shape
-    shared = mate_ref.shape[0]
+def pick_body(m_ref, s_ref, high_ref, low_ref):
+    def step(j, carry):
+        at = pl.ds(pl.multiple_of(j * ROWS, ROWS), ROWS)
+        rows = jnp.zeros((s_ref.shape[1], ROWS), F32)
+        for i in range(s_ref.shape[0]):
+            part = m_ref[i * ROWS:(i + 1) * ROWS, at]
+            high, low = halves(part)
+            tail = (part - high.astype(F32) - low.astype(F32)).astype(BF16)
+            pick = s_ref[i]
+            rows = rows + (fast(pick, high) + fast(pick, low) + fast(pick, tail))
+        high_ref[:, at], low_ref[:, at] = halves(rows)
+        return carry
+
+    lax.fori_loop(0, m_ref.shape[1] // ROWS, step, 0)
+
+
+def multiply_body(m_ref, x_ref, high_ref, low_ref, out_ref, part_ref):
     xh, xl = high_ref[...], low_ref[...]
 
-    def step(at, i, carry):
-        part, sent = carry
+    def step(at, i, part):
         mh, ml = halves(m_ref[at, :])
         out = fast(mh, xh) + fast(mh, xl) + fast(ml, xh)
         out_ref[at, :] = out
-        part = part + jnp.sum(x_ref[at, :] * out, axis=0, keepdims=True)
-        uh, ul = halves(out)
-        pick = s_ref[i]
-        return part, sent + fast(pick, uh) + fast(pick, ul)
-
-    start = (jnp.zeros((1, cases), F32), jnp.zeros((2 * shared, cases), F32))
-    part, sent = blocks_of(rows, step, start)
-    part_ref[...] = part
+        return part + jnp.sum(x_ref[at, :] * out, axis=0, keepdims=True)
+
+    part = blocks_of(out_ref.shape[0], step, jnp.zeros((1, out_ref.shape[1]), F32))
+    copied(part_ref, part)
+
+
+def copied(ref, row):
+    if len(ref.shape) == 2:
+        ref[...] = row
+        return
+    for member in range(ref.shape[0]):
+        ref[member] = row
+
+
+def relay_body(near_ref, out_ref):
+    copied(out_ref, summed(near_ref))
+
+
+def keep(at, x, outs):
+    x_ref, high_ref, low_ref = outs[2:5]
+    x_ref[at, :] = x
+    high_ref[at, :], low_ref[at, :] = halves(x)
+
+
+def send(edge_high_ref, edge_low_ref, outs):
+    mate_ref, far_ref, _, high_ref, low_ref = outs[:5]
+    xh, xl, mh = high_ref[...], low_ref[...], edge_high_ref[...]
+    sent = fast(mh, xh) + fast(mh, xl) + fast(edge_low_ref[...], xh)
+    shared = mate_ref.shape[0]
     mate_ref[...] = sent[:shared]
     far_ref[...] = sent[shared:]
 
 
-def keep(at, x, x_ref, high_ref, low_ref):
-    x_ref[at, :] = x
-    high_ref[at, :], low_ref[at, :] = halves(x)
-
-
-def precondition_first(near_ref, r_ref, w_ref, rt_ref, m_ref, s_ref,
-                       out_ref, mate_ref, far_ref, part_ref, total_ref, x_ref, high_ref, low_ref):
+def precondition_first(near_ref, edge_high_ref, edge_low_ref, rt_ref, r_ref, w_ref, *outs):
     total = summed(near_ref)
-    total_ref[...] = total
+    outs[5][...] = total
     amounts = stacked(total)
 
     def step(at, i, carry):
-        keep(at, w_ref[at, :] * (r_ref[at, :] - fast(rt_ref[at, :], amounts)), x_ref, high_ref, low_ref)
+        keep(at, w_ref[at, :] * (r_ref[at, :] - fast(rt_ref[at, :], amounts)), outs)
         return carry
 
     blocks_of(r_ref.shape[0], step, 0)
-    multiply(m_ref, s_ref, x_ref, high_ref, low_ref, out_ref, mate_ref, far_ref, part_ref)
-
-
-def direct_first(near_ref, v_ref, rt_ref, m_ref, s_ref,
-                 out_ref, mate_ref, far_ref, part_ref, total_ref, x_ref, high_ref, low_ref):
+    send(edge_high_ref, edge_low_ref, outs)
+
+
+def direct_first(near_ref, edge_high_ref, edge_low_ref, rt_ref, v_ref, *outs):
     total = summed(near_ref)
-    total_ref[...] = total
+    outs[5][...] = total
     amounts = stacked(total)
 
     def step(at, i, carry):
-        keep(at, v_ref[at, :] - fast(rt_ref[at, :], amounts), x_ref, high_ref, low_ref)
+        keep(at, v_ref[at, :] - fast(rt_ref[at, :], amounts), outs)
         return carry
 
     blocks_of(v_ref.shape[0], step, 0)
-    multiply(m_ref, s_ref, x_ref, high_ref, low_ref, out_ref, mate_ref, far_ref, part_ref)
-
-
-def precondition_next(modes, near_ref, before_ref, norm_ref, r_ref, image_ref, w_ref, rt_ref, m_ref, s_ref,
-                      out_ref, mate_ref, far_ref, part_ref, size_ref, r_out_ref, step_ref, x_ref, high_ref, low_ref):
+    send(edge_high_ref, edge_low_ref, outs)
+
+
+def precondition_next(modes, near_ref, edge_high_ref, edge_low_ref, rt_ref, before_ref, norm_ref, r_ref, image_ref,
+                      w_ref, *outs):
+    size_ref, r_out_ref, step_ref = outs[5:]
     total = summed(near_ref)
     length = norm_ref[modes:modes + 1, :] / total[modes:modes + 1]
     step_ref[...] = length
@@ -140,27 +168,28 @@
         residual = r_ref[at, :] - length * image_ref[at, :]
         r_out_ref[at, :] = residual
         weighted = w_ref[at, :] * residual
-        keep(at, w_ref[at, :] * (residual - fast(rt_ref[at, :], amounts)), x_ref, high_ref, low_ref)
+        keep(at, w_ref[at, :] * (residual - fast(rt_ref[at, :], amounts)), outs)
         return size + jnp.sum(weighted * residual, axis=0, keepdims=True)
 
     size_ref[...] = blocks_of(r_ref.shape[0], step, jnp.zeros((1, r_ref.shape[1]), F32))
-    multiply(m_ref, s_ref, x_ref, high_ref, low_ref, out_ref, mate_ref, far_ref, part_ref)
-
-
-def direct_next(modes, near_ref, norm_ref, v_ref, d_ref, rt_ref, m_ref, s_ref,
-                out_ref, mate_ref, far_ref, part_ref, total_ref, x_ref, high_ref, low_ref):
+    send(edge_high_ref, edge_low_ref, outs)
+
+
+def direct_next(modes, near_ref, edge_high_ref, edge_low_ref, rt_ref, norm_ref, first_ref, v_ref, d_ref, *outs):
     total = summed(near_ref)
-    total_ref[...] = total
+    outs[5][...] = total
+    outs[6][0:1, :] = first_ref[modes:modes + 1, :]
+    outs[6][1:2, :] = total[modes + 1:modes + 2]
     ratio = total[modes:modes + 1] / norm_ref[modes:modes + 1, :]
     amounts = stacked(total)
 
     def step(at, i, carry):
         update = v_ref[at, :] - fast(rt_ref[at, :], amounts)
-        keep(at, update + ratio * d_ref[at, :], x_ref, high_ref, low_ref)
+        keep(at, update + ratio * d_ref[at, :], outs)
         return carry
 
     blocks_of(v_ref.shape[0], step, 0)
-    multiply(m_ref, s_ref, x_ref, high_ref, low_ref, out_ref, mate_ref, far_ref, part_ref)
+    send(edge_high_ref, edge_low_ref, outs)
 
 
 def received(mate_ref, far_ref):
@@ -314,10 +343,11 @@
     out_ref[...] = out.reshape(out_ref.shape)
 
 
-def finish_body(q_ref, mate_ref, far_ref, st_ref, r_ref, first_ref, second_ref, step_first_ref, step_ref,
-                multipliers_ref, residual_ref):
+def finish_body(modes, q_ref, mate_ref, far_ref, st_ref, r_ref, first_ref, second_ref, step_first_ref, last_ref,
+                bending_ref, multipliers_ref, residual_ref):
     rh, rl = received(mate_ref, far_ref)
-    first, second = step_first_ref[...], step_ref[...]
+    first = step_first_ref[...]
+    second = last_ref[modes:modes + 1, :] / summed(bending_ref)
 
     def step(at, i, carry):
         place = st_ref[at, :]
@@ -363,8 +393,6 @@
     row = (1, cases)
     rows_out = (3 * TILE, cases)
     pack_shape = (inner, TILE, cases)
-    scratch = [pltpu.VMEM(field, F32), pltpu.VMEM(field, BF16), pltpu.VMEM(field, BF16)]
-    own = scratch[1:]
     big = 6 * local_rows * local_rows * cases
     light = 4 * local_rows * cases * 2 * shared
     moved = 4 * local_rows * (local_rows + 3 * cases)
@@ -379,13 +407,19 @@
         [payload, payload, shaped((local_rows // ROWS, 2 * TILE, ROWS), BF16)], [], light, 8 * local_rows * cases,
     )(gap_raw, jnp.pad(coarse_rows, pad), jnp.pad(rigid_images, pad), selector)
     from_mate, from_far = exchanged(to_mate, to_far)
-    from_mate, from_far, placer, weights = lax.optimization_barrier((from_mate, from_far, placer, weights))
+    edges = [
+        call(pick_body, [shaped((2 * shared, local_rows), BF16)] * 2, [], light, 4 * local_rows * local_rows)(m, selector)
+        for m in (boundary_solve_blocks, dual_ops)
+    ]
+    from_mate, from_far, placer, weights, edges = lax.optimization_barrier(
+        (from_mate, from_far, placer, weights, edges)
+    )
     [block] = call(
         functools.partial(tile_body, modes, shared), [(outer, 3 * TILE, inner * TILE)], [], 1, 8 * local_rows
     )(to_mate, from_mate, from_far)
     block = swap(block, OUTER)
-    block, from_mate, from_far, placer, weights = lax.optimization_barrier(
-        (block, from_mate, from_far, placer, weights)
+    block, from_mate, from_far, placer, weights, edges = lax.optimization_barrier(
+        (block, from_mate, from_far, placer, weights, edges)
     )
 
     def coarse(pack):
@@ -402,33 +436,38 @@
         functools.partial(start_body, modes), [field, pack_shape, shaped((local_rows, 128), BF16)], [], light,
         12 * local_rows * cases,
     )(gap_raw, from_mate, from_far, placer, weights, rigid_wide)
+    sent = [edge, edge, field, shaped(field, BF16), shaped(field, BF16)]
+
+    def advance(body, extra, near, which, *operands, parts=row):
+        to_mate, to_far, x, high, low, *rest = call(
+            body, sent + extra, [], light, 12 * local_rows * cases
+        )(near, *edges[which], rigid_tall, *operands)
+        out, part = call(multiply_body, [field, parts], [], big, moved)(
+            (boundary_solve_blocks, dual_ops)[which], x, high, low
+        )
+        return out, exchanged(to_mate, to_far), part, x, *rest
+
     near = coarse(pack)
-    out, to_mate, to_far, part, amounts = call(
-        precondition_first, [field, edge, edge, row, rows_out], scratch, big, moved
-    )(near, residual, weights, rigid_tall, boundary_solve_blocks, selector)
-    norm_first = amounts[modes]
-    smoothed, pack = assemble(True, False, out, *exchanged(to_mate, to_far), placer, rigid_wide, part, weights)
+    out, received_rows, part, _, amounts = advance(precondition_first, [rows_out], near, 0, residual, weights)
+    smoothed, pack = assemble(True, False, out, *received_rows, placer, rigid_wide, part, weights)
     near = coarse(pack)
-    out, to_mate, to_far, part, total, direction_first = call(
-        direct_first, [field, edge, edge, row, rows_out, field], own, big, moved
-    )(near, smoothed, rigid_tall, dual_ops, selector)
-    image, pack = assemble(False, False, out, *exchanged(to_mate, to_far), placer, rigid_wide, part)
+    out, received_rows, part, direction_first, total = advance(direct_first, [rows_out], near, 1, smoothed)
+    image, pack = assemble(False, False, out, *received_rows, placer, rigid_wide, part)
     near = coarse(pack)
-    out, to_mate, to_far, part, size, residual, step_first = call(
-        functools.partial(precondition_next, modes), [field, edge, edge, row, row, field, row], scratch, big, moved
-    )(near, amounts, total, residual, image, weights, rigid_tall, boundary_solve_blocks, selector)
-    smoothed, pack = assemble(True, True, out, *exchanged(to_mate, to_far), placer, rigid_wide, part, weights, size)
+    out, received_rows, part, _, size, residual, step_first = advance(
+        functools.partial(precondition_next, modes), [row, field, row], near, 0, amounts, total, residual, image, weights
+    )
+    smoothed, pack = assemble(True, True, out, *received_rows, placer, rigid_wide, part, weights, size)
     near = coarse(pack)
-    out, to_mate, to_far, part, last, direction = call(
-        functools.partial(direct_next, modes), [field, edge, edge, row, rows_out, field], own, big, moved
-    )(near, total, smoothed, direction_first, rigid_tall, dual_ops, selector)
-    norms = jnp.stack([norm_first, last[modes + 1]])
-    from_mate, from_far = exchanged(to_mate, to_far)
-    part, from_mate, from_far, norms = lax.optimization_barrier((part, from_mate, from_far, norms))
-    bending = jnp.sum(swap(jnp.broadcast_to(part, (count, 1, cases)), CLUSTER_SUB), axis=0)
-    step = last[modes:modes + 1] / bending
-    multipliers, residual = call(finish_body, [field, field], [], light, 24 * local_rows * cases)(
-        out, from_mate, from_far, placer, residual, direction_first, direction, step_first, step
+    out, (from_mate, from_far), part, direction, last, norms = advance(
+        functools.partial(direct_next, modes), [rows_out, (2, cases)], near, 1, total, amounts, smoothed, direction_first,
+        parts=(inner, 1, cases),
+    )
+    part, norms, from_mate, from_far = lax.optimization_barrier((part, norms, from_mate, from_far))
+    [part] = call(relay_body, [(outer, 1, cases)], [], 1, 4 * outer * cases)(swap(part, INNER))
+    bending = swap(part, OUTER)
+    multipliers, residual = call(functools.partial(finish_body, modes), [field, field], [], light, 24 * local_rows * cases)(
+        out, from_mate, from_far, placer, residual, direction_first, direction, step_first, last, bending
     )
     return (multipliers, residual, norms)
 

time: 233 us -> 215 us (0.923)
  waiting for transfers between devices: 21 us -> 7.09 us
  starting transfers between devices: 20.1 us -> 15.5 us
    ppermute x10, waiting for transfers between devices: 21 us -> 7.09 us  [matched(): return lax.ppermute(value, CLUSTER_SUB, pairs)]
    ppermute x10, starting transfers between devices: 20.1 us -> 15.5 us  [matched(): return lax.ppermute(value, CLUSTER_SUB, pairs)]
    pallas_call x15 -> x22, Pallas kernels: 31.1 us -> 33.3 us  [run(): pl.pallas_call(body, out_shape=[s if hasattr(s, 'dtype') else jax.ShapeDt...]
    unnamed x16 -> x10, local copies, waits for them, and re-layouts: 5.61 us -> 3.65 us
    all_to_all x10 -> x11, blocking collectives: 150 us -> 151 us  [swap(): return lax.all_to_all(blocks, axis, split_axis=0, concat_axis=0, tiled=True)]
  transfers between devices with their start and end apart: 10 -> 10, of which waited for: 5 -> 4; matrix products, arithmetic and copies ran while one was open for 0% -> 0% of each run, Pallas kernels for 0% -> 7%
where the time goes in v2:
time: 215 us; the launch traced here: 214 us
  blocking collectives  151 us (70%)
  Pallas kernels  33.3 us (15%)
  starting transfers between devices  15.5 us (7%)
  waiting for transfers between devices  7.09 us (3%)
  local copies, waits for them, and re-layouts  5.43 us (3%)
    all_to_all x11, blocking collectives, swap(): return lax.all_to_all(blocks, axis, split_axis=0, concat_axis=0, tiled=True)  151 us
    pallas_call x22, Pallas kernels, run(): pl.pallas_call(body, out_shape=[s if hasattr(s, 'dtype') else jax.ShapeDt...  33.3 us
    ppermute x10, starting transfers between devices, matched(): return lax.ppermute(value, CLUSTER_SUB, pairs)  15.5 us
    ppermute x10, waiting for transfers between devices, matched(): return lax.ppermute(value, CLUSTER_SUB, pairs)  7.09 us
  transfers between devices with their start and end apart: 10, of which 4 were waited for; matrix products, arithmetic and copies ran while one was open for 0% of the time, Pallas kernels for 7%

profile of v2, /device:TPU:1, one launch (start us, length us, event | category | flops | bytes accessed | tf_op | source)
XLA Modules:
  0.0 214.3 jit_solution(9001643063483761203)
XLA Ops:
  0.7 0.8 pad.10.rigid_ref
  1.4 0.8 pad.9.coarse_ref
  2.3 0.9 fusion
  3.1 0.2 select_convert_fusion.1.s_ref
  3.3 0.0 copy-start.3
  3.3 1.4 copy-done.3
  4.8 1.6 shard_map.85
  6.4 3.0 %collective-permute-start.1 = (f32[200,256]{1,0:T(8,128)S(1)}, f32[200,256]{1,0:T(8,128)S(1)}, u32[]{:S(2)}, u32[]{:S(2)}) collective-permute-start(f32[200,256]{1,0:T(8,128)S(1)} %get-tuple-element.78), channel_id=1, source_target_pairs={{0,255},{1,2},{2,1},{3,4},{4,3},{5,6},{6,5},{7,8},{8,7},{9,10},{10... | collective-permute-start | bytes 614408 | tf_op jit(solution)/shard_map/ppermute | solution.py:36
  9.4 8.4 %collective-permute-start = (f32[200,256]{1,0:T(8,128)S(1)}, f32[200,256]{1,0:T(8,128)S(1)}, u32[]{:S(2)}, u32[]{:S(2)}) collective-permute-start(f32[200,256]{1,0:T(8,128)S(1)} %get-tuple-element.77.own_ref), channel_id=1, source_target_pairs={{0,1},{1,0},{2,3},{3,2},{4,5},{5,4},{6,7},{7,6},{8,9},{9,8},{10,11... | collective-permute-start | bytes 614408 | tf_op jit(solution)/shard_map/ppermute | solution.py:36
  17.8 0.2 select_reduce_fusion
  18.0 0.2 select_convert_fusion.st_ref.refs_3_
  18.2 0.0 copy-start.1
  18.2 2.2 %copy-done.1 = f32[1024,1024]{1,0:T(8,128)S(1)} copy-done((f32[1024,1024]{1,0:T(8,128)S(1)}, f32[1024,1024]{1,0:T(8,128)}, u32[]{:S(2)}) %copy-start.1) | copy-done | bytes 4194328
  20.4 2.5 %shard_map.87 = (bf16[256,1024]{1,0:T(8,128)(2,1)S(1)}, bf16[256,1024]{1,0:T(8,128)(2,1)S(1)}) custom-call(f32[1024,1024]{1,0:T(8,128)S(1)} %copy-done.1, bf16[4,256,256]{2,1,0:T(8,128)(2,1)S(1)} %select_convert_fusion.1.s_ref), custom_call_target="tpu_custom_call" | custom-call | flops 268435456 | bytes 4194304 | tf_op jit(solution)/shard_map/pallas_call | solution.py:47
  22.9 0.0 copy-start.4
  23.0 2.5 %shard_map.86 = (bf16[256,1024]{1,0:T(8,128)(2,1)S(1)}, bf16[256,1024]{1,0:T(8,128)(2,1)S(1)}) custom-call(f32[1024,1024]{1,0:T(8,128)S(1)} %copy-done, bf16[4,256,256]{2,1,0:T(8,128)(2,1)S(1)} %select_convert_fusion.1.s_ref), custom_call_target="tpu_custom_call" | custom-call | flops 268435456 | bytes 4194304 | tf_op jit(solution)/shard_map/pallas_call | solution.py:47
  25.5 0.0 collective-permute-done.1.far_ref
  25.5 0.0 collective-permute-done.mate_ref
  25.5 0.2 broadcast_in_dim.43.w_ref.refs_6_
  25.8 10.1 %all_to_all.55.block_ref = f32[16,24,128]{2,1,0:T(8,128)S(1)} all-to-all(f32[16,24,128]{2,1,0:T(8,128)S(1)} %shard_map.88), channel_id=1, replica_groups=mesh['cluster'=4,'sub_0'=4,'sub_1'=8,'sub_2'=2] {'cluster','sub_0'}, dimensions={0} | all-to-all | bytes 393216 | tf_op jit(solution)/shard_map/all_to_all | solution.py:32
  35.9 2.1 shard_map.89
  38.0 13.3 %all_to_all.56.near_ref = f32[16,8,256]{2,1,0:T(8,128)S(1)} all-to-all(f32[16,8,256]{2,1,0:T(8,128)S(1)} %get-tuple-element.97), channel_id=1, replica_groups=mesh['cluster'=4,'sub_0'=4,'sub_1'=8,'sub_2'=2] {'sub_1','sub_2'}, dimensions={0} | all-to-all | bytes 262144 | tf_op jit(solution)/shard_map/all_to_all | solution.py:32
  51.2 0.3 shard_map.90
  51.5 12.2 %all_to_all.57.near_ref = f32[16,24,256]{2,1,0:T(8,128)S(1)} all-to-all(f32[16,24,256]{2,1,0:T(8,128)S(1)} %shard_map.90), channel_id=1, replica_groups=mesh['cluster'=4,'sub_0'=4,'sub_1'=8,'sub_2'=2] {'cluster','sub_0'}, dimensions={0} | all-to-all | bytes 786432 | tf_op jit(solution)/shard_map/all_to_all | solution.py:32
  63.7 1.4 shard_map.91
  65.1 1.8 collective-permute-start.2
  66.9 0.3 collective-permute-start.3
  67.2 2.5 %shard_map.92 = (f32[1024,256]{1,0:T(8,128)S(1)}, f32[1,256]{1,0:T(1,128)S(1)}) custom-call(f32[1024,1024]{1,0:T(8,128)S(1)} %copy-done, f32[1024,256]{1,0:T(8,128)S(1)} %get-tuple-element.102.x_ref, bf16[1024,256]{1,0:T(8,128)(2,1)S(1)} %get-tuple-element.103.high_ref, bf16[1024,256]{1,0:T(8,128)(2,1)S(1)} %get-tuple-element.104.low_ref), custom_call_target="tpu_custom_call" | custom-call | flops 1610612736 | bytes 7340032 | tf_op jit(solution)/shard_map/pallas_call | solution.py:47
  69.7 0.0 copy-start.2
  69.7 0.0 collective-permute-done.2.refs_1_
  69.7 1.5 collective-permute-done.3.refs_2_
  71.3 1.8 shard_map.93
  73.1 17.1 %all_to_all.58.near_ref = f32[16,8,256]{2,1,0:T(8,128)S(1)} all-to-all(f32[16,8,256]{2,1,0:T(8,128)S(1)} %get-tuple-element.109), channel_id=1, replica_groups=mesh['cluster'=4,'sub_0'=4,'sub_1'=8,'sub_2'=2] {'sub_1','sub_2'}, dimensions={0} | all-to-all | bytes 262144 | tf_op jit(solution)/shard_map/all_to_all | solution.py:32
  90.2 0.3 shard_map.94
  90.5 13.1 %all_to_all.59.near_ref = f32[16,24,256]{2,1,0:T(8,128)S(1)} all-to-all(f32[16,24,256]{2,1,0:T(8,128)S(1)} %shard_map.94), channel_id=1, replica_groups=mesh['cluster'=4,'sub_0'=4,'sub_1'=8,'sub_2'=2] {'cluster','sub_0'}, dimensions={0} | all-to-all | bytes 786432 | tf_op jit(solution)/shard_map/all_to_all | solution.py:32
  103.6 1.4 shard_map.95
  105.0 0.6 collective-permute-start.4
  105.5 0.0 collective-permute-start.5
  105.6 2.5 %shard_map.96 = (f32[1024,256]{1,0:T(8,128)S(1)}, f32[1,256]{1,0:T(1,128)S(1)}) custom-call(f32[1024,1024]{1,0:T(8,128)S(1)} %copy-done.2, f32[1024,256]{1,0:T(8,128)S(1)} %get-tuple-element.113.x_ref.d_ref.first_ref, bf16[1024,256]{1,0:T(8,128)(2,1)S(1)} %get-tuple-element.114.high_ref, bf16[1024,256]{1,0:T(8,128)(2,1)S(1)} %get-tuple-element.115.low_ref), custom_call_target="tpu_custom_call" | custom-call | flops 1610612736 | bytes 7340032 | tf_op jit(solution)/shard_map/pallas_call | solution.py:47
  108.1 0.0 collective-permute-done.4.refs_1_
  108.1 1.8 collective-permute-done.5.refs_2_
  109.9 1.8 shard_map.97
  111.7 17.1 %all_to_all.60.near_ref = f32[16,8,256]{2,1,0:T(8,128)S(1)} all-to-all(f32[16,8,256]{2,1,0:T(8,128)S(1)} %get-tuple-element.120), channel_id=1, replica_groups=mesh['cluster'=4,'sub_0'=4,'sub_1'=8,'sub_2'=2] {'sub_1','sub_2'}, dimensions={0} | all-to-all | bytes 262144 | tf_op jit(solution)/shard_map/all_to_all | solution.py:32
  128.8 0.3 shard_map.98
  129.1 13.1 %all_to_all.61.near_ref = f32[16,24,256]{2,1,0:T(8,128)S(1)} all-to-all(f32[16,24,256]{2,1,0:T(8,128)S(1)} %shard_map.98), channel_id=1, replica_groups=mesh['cluster'=4,'sub_0'=4,'sub_1'=8,'sub_2'=2] {'cluster','sub_0'}, dimensions={0} | all-to-all | bytes 786432 | tf_op jit(solution)/shard_map/all_to_all | solution.py:32
  142.3 1.4 shard_map.99
  143.7 0.8 collective-permute-start.6
  144.5 0.0 collective-permute-start.7
  144.5 2.5 %shard_map.100 = (f32[1024,256]{1,0:T(8,128)S(1)}, f32[1,256]{1,0:T(1,128)S(1)}) custom-call(f32[1024,1024]{1,0:T(8,128)S(1)} %copy-done, f32[1024,256]{1,0:T(8,128)S(1)} %get-tuple-element.124.x_ref, bf16[1024,256]{1,0:T(8,128)(2,1)S(1)} %get-tuple-element.125.high_ref, bf16[1024,256]{1,0:T(8,128)(2,1)S(1)} %get-tuple-element.126.low_ref), custom_call_target="tpu_custom_call" | custom-call | flops 1610612736 | bytes 7340032 | tf_op jit(solution)/shard_map/pallas_call | solution.py:47
  147.0 0.0 collective-permute-done.6.refs_1_
  147.0 1.8 collective-permute-done.7.refs_2_
  148.9 1.8 shard_map.101
  150.7 17.1 %all_to_all.62.near_ref = f32[16,8,256]{2,1,0:T(8,128)S(1)} all-to-all(f32[16,8,256]{2,1,0:T(8,128)S(1)} %get-tuple-element.132), channel_id=1, replica_groups=mesh['cluster'=4,'sub_0'=4,'sub_1'=8,'sub_2'=2] {'sub_1','sub_2'}, dimensions={0} | all-to-all | bytes 262144 | tf_op jit(solution)/shard_map/all_to_all | solution.py:32
  167.8 0.3 shard_map.102
  168.1 13.1 %all_to_all.63.near_ref = f32[16,24,256]{2,1,0:T(8,128)S(1)} all-to-all(f32[16,24,256]{2,1,0:T(8,128)S(1)} %shard_map.102), channel_id=1, replica_groups=mesh['cluster'=4,'sub_0'=4,'sub_1'=8,'sub_2'=2] {'cluster','sub_0'}, dimensions={0} | all-to-all | bytes 786432 | tf_op jit(solution)/shard_map/all_to_all | solution.py:32
  181.2 1.4 shard_map.103
  182.6 0.6 collective-permute-start.8
  183.2 0.0 collective-permute-start.9
  183.2 2.5 %shard_map.104 = (f32[1024,256]{1,0:T(8,128)S(1)}, f32[16,1,256]{2,1,0:T(1,128)S(1)}) custom-call(f32[1024,1024]{1,0:T(8,128)S(1)} %copy-done.2, f32[1024,256]{1,0:T(8,128)S(1)} %get-tuple-element.134.x_ref.second_ref, bf16[1024,256]{1,0:T(8,128)(2,1)S(1)} %get-tuple-element.135.high_ref, bf16[1024,256]{1,0:T(8,128)(2,1)S(1)} %get-tuple-element.136.low_ref), custom_call_target="tpu_custom_call" | custom-call | flops 1610612736 | bytes 7340032 | tf_op jit(solution)/shard_map/pallas_call | solution.py:47
  185.8 0.0 collective-permute-done.8.mate_ref
  185.8 1.8 collective-permute-done.9.far_ref
  187.6 15.3 %all_to_all.64.near_ref = f32[16,1,256]{2,1,0:T(1,128)S(1)} all-to-all(f32[16,1,256]{2,1,0:T(1,128)S(1)} %get-tuple-element.147), channel_id=1, replica_groups=mesh['cluster'=4,'sub_0'=4,'sub_1'=8,'sub_2'=2] {'sub_1','sub_2'}, dimensions={0} | all-to-all | bytes 32768 | tf_op jit(solution)/shard_map/all_to_all | solution.py:32
  202.9 9.0 %all_to_all.65.bending_ref = f32[16,1,256]{2,1,0:T(1,128)S(1)} all-to-all(f32[16,1,256]{2,1,0:T(1,128)S(1)} %shard_map.105), channel_id=1, replica_groups=mesh['cluster'=4,'sub_0'=4,'sub_1'=8,'sub_2'=2] {'cluster','sub_0'}, dimensions={0} | all-to-all | bytes 32768 | tf_op jit(solution)/shard_map/all_to_all | solution.py:32
  211.9 2.4 %shard_map.106 = (f32[1024,256]{1,0:T(8,128)}, f32[1024,256]{1,0:T(8,128)}) custom-call(f32[1024,256]{1,0:T(8,128)S(1)} %get-tuple-element.137.q_ref, f32[128,256]{1,0:T(8,128)S(1)} %collective-permute-done.8.mate_ref, f32[128,256]{1,0:T(8,128)S(1)} %collective-permute-done.9.far_ref, bf16[1024,256]{1,0:T(8,128)(2,1)S(1)} %select_convert_fusion.st_ref.refs_3_, ...), custom_call_target="tpu_custom_call" | custom-call | flops 268435456 | bytes 6291456 | tf_op jit(solution)/shard_map/pallas_call | solution.py:47
  (11 shorter events, 0.1 us)
Async XLA Ops:
  2.2 20.7 %copy-start = (f32[1024,1024]{1,0:T(8,128)S(1)}, f32[1024,1024]{1,0:T(8,128)}, u32[]{:S(2)}) copy-start(f32[1024,1024]{1,0:T(8,128)} %m_ref.10) | copy-start | bytes 12582916
  3.3 1.5 copy-start.3
  6.4 19.2 %collective-permute-start.1 = (f32[200,256]{1,0:T(8,128)S(1)}, f32[200,256]{1,0:T(8,128)S(1)}, u32[]{:S(2)}, u32[]{:S(2)}) collective-permute-start(f32[200,256]{1,0:T(8,128)S(1)} %get-tuple-element.78), channel_id=1, source_target_pairs={{0,255},{1,2},{2,1},{3,4},{4,3},{5,6},{6,5},{7,8},{8,7},{9,10},{10... | collective-permute-start | bytes 614408 | tf_op jit(solution)/shard_map/ppermute | solution.py:36
  9.4 16.1 %collective-permute-start = (f32[200,256]{1,0:T(8,128)S(1)}, f32[200,256]{1,0:T(8,128)S(1)}, u32[]{:S(2)}, u32[]{:S(2)}) collective-permute-start(f32[200,256]{1,0:T(8,128)S(1)} %get-tuple-element.77.own_ref), channel_id=1, source_target_pairs={{0,1},{1,0},{2,3},{3,2},{4,5},{5,4},{6,7},{7,6},{8,9},{9,8},{10,11... | collective-permute-start | bytes 614408 | tf_op jit(solution)/shard_map/ppermute | solution.py:36
  18.2 2.2 %copy-start.1 = (f32[1024,1024]{1,0:T(8,128)S(1)}, f32[1024,1024]{1,0:T(8,128)}, u32[]{:S(2)}) copy-start(f32[1024,1024]{1,0:T(8,128)} %m_ref.11) | copy-start | bytes 12582916
  22.9 12.9 %copy-start.4 = (f32[1024,256]{1,0:T(8,128)S(1)}, f32[1024,256]{1,0:T(8,128)}, u32[]{:S(2)}) copy-start(f32[1024,256]{1,0:T(8,128)} %y_ref.1) | copy-start | bytes 3145732
  65.1 4.6 %collective-permute-start.2 = (f32[128,256]{1,0:T(8,128)S(1)}, f32[128,256]{1,0:T(8,128)S(1)}, u32[]{:S(2)}, u32[]{:S(2)}) collective-permute-start(f32[128,256]{1,0:T(8,128)S(1)} %get-tuple-element.106), channel_id=1, source_target_pairs={{0,1},{1,0},{2,3},{3,2},{4,5},{5,4},{6,7},{7,6},{8,9},{9,8},{10,11... | collective-permute-start | bytes 393224 | tf_op jit(solution)/shard_map/ppermute | solution.py:36
  66.9 4.4 %collective-permute-start.3 = (f32[128,256]{1,0:T(8,128)S(1)}, f32[128,256]{1,0:T(8,128)S(1)}, u32[]{:S(2)}, u32[]{:S(2)}) collective-permute-start(f32[128,256]{1,0:T(8,128)S(1)} %get-tuple-element.107), channel_id=1, source_target_pairs={{0,255},{1,2},{2,1},{3,4},{4,3},{5,6},{6,5},{7,8},{8,7},{9,10},{10... | collective-permute-start | bytes 393224 | tf_op jit(solution)/shard_map/ppermute | solution.py:36
  69.7 35.9 %copy-start.2 = (f32[1024,1024]{1,0:T(8,128)S(1)}, f32[1024,1024]{1,0:T(8,128)}, u32[]{:S(2)}) copy-start(f32[1024,1024]{1,0:T(8,128)} %m_ref.11) | copy-start | bytes 12582916
  105.0 3.1 %collective-permute-start.4 = (f32[128,256]{1,0:T(8,128)S(1)}, f32[128,256]{1,0:T(8,128)S(1)}, u32[]{:S(2)}, u32[]{:S(2)}) collective-permute-start(f32[128,256]{1,0:T(8,128)S(1)} %get-tuple-element.117), channel_id=1, source_target_pairs={{0,1},{1,0},{2,3},{3,2},{4,5},{5,4},{6,7},{7,6},{8,9},{9,8},{10,11... | collective-permute-start | bytes 393224 | tf_op jit(solution)/shard_map/ppermute | solution.py:36
  105.5 4.4 %collective-permute-start.5 = (f32[128,256]{1,0:T(8,128)S(1)}, f32[128,256]{1,0:T(8,128)S(1)}, u32[]{:S(2)}, u32[]{:S(2)}) collective-permute-start(f32[128,256]{1,0:T(8,128)S(1)} %get-tuple-element.118), channel_id=1, source_target_pairs={{0,255},{1,2},{2,1},{3,4},{4,3},{5,6},{6,5},{7,8},{8,7},{9,10},{10... | collective-permute-start | bytes 393224 | tf_op jit(solution)/shard_map/ppermute | solution.py:36
  143.7 3.3 %collective-permute-start.6 = (f32[128,256]{1,0:T(8,128)S(1)}, f32[128,256]{1,0:T(8,128)S(1)}, u32[]{:S(2)}, u32[]{:S(2)}) collective-permute-start(f32[128,256]{1,0:T(8,128)S(1)} %get-tuple-element.128), channel_id=1, source_target_pairs={{0,1},{1,0},{2,3},{3,2},{4,5},{5,4},{6,7},{7,6},{8,9},{9,8},{10,11... | collective-permute-start | bytes 393224 | tf_op jit(solution)/shard_map/ppermute | solution.py:36
  144.5 4.4 %collective-permute-start.7 = (f32[128,256]{1,0:T(8,128)S(1)}, f32[128,256]{1,0:T(8,128)S(1)}, u32[]{:S(2)}, u32[]{:S(2)}) collective-permute-start(f32[128,256]{1,0:T(8,128)S(1)} %get-tuple-element.129), channel_id=1, source_target_pairs={{0,255},{1,2},{2,1},{3,4},{4,3},{5,6},{6,5},{7,8},{8,7},{9,10},{10... | collective-permute-start | bytes 393224 | tf_op jit(solution)/shard_map/ppermute | solution.py:36
  182.6 3.1 %collective-permute-start.8 = (f32[128,256]{1,0:T(8,128)S(1)}, f32[128,256]{1,0:T(8,128)S(1)}, u32[]{:S(2)}, u32[]{:S(2)}) collective-permute-start(f32[128,256]{1,0:T(8,128)S(1)} %get-tuple-element.140), channel_id=1, source_target_pairs={{0,1},{1,0},{2,3},{3,2},{4,5},{5,4},{6,7},{7,6},{8,9},{9,8},{10,11... | collective-permute-start | bytes 393224 | tf_op jit(solution)/shard_map/ppermute | solution.py:36
  183.2 4.4 %collective-permute-start.9 = (f32[128,256]{1,0:T(8,128)S(1)}, f32[128,256]{1,0:T(8,128)S(1)}, u32[]{:S(2)}, u32[]{:S(2)}) collective-permute-start(f32[128,256]{1,0:T(8,128)S(1)} %get-tuple-element.141), channel_id=1, source_target_pairs={{0,255},{1,2},{2,1},{3,4},{4,3},{5,6},{6,5},{7,8},{8,7},{9,10},{10... | collective-permute-start | bytes 393224 | tf_op jit(solution)/shard_map/ppermute | solution.py:36

commit v3 on v2

--- a/solution.py
+++ b/solution.py
@@ -14,6 +14,7 @@
 TILE = 8
 ROWS = 256
 VMEM_LIMIT = 24 * 1024 * 1024
+LARGE_LIMIT = 66000000
 
 F32 = jnp.float32
 BF16 = jnp.bfloat16
@@ -42,15 +43,16 @@
     return near, far
 
 
-def call(body, out_shapes, scratch, flops, moved):
+def call(body, out_shapes, scratch, flops, moved, outside=0, limit=VMEM_LIMIT):
     def run(*operands):
         return pl.pallas_call(
             body,
             out_shape=[s if hasattr(s, "dtype") else jax.ShapeDtypeStruct(s, F32) for s in out_shapes],
-            in_specs=[pl.BlockSpec(memory_space=pltpu.VMEM)] * len(operands),
+            in_specs=[pl.BlockSpec(memory_space=pltpu.HBM)] * outside
+            + [pl.BlockSpec(memory_space=pltpu.VMEM)] * (len(operands) - outside),
             out_specs=[pl.BlockSpec(memory_space=pltpu.VMEM)] * len(out_shapes),
             scratch_shapes=scratch,
-            compiler_params=pltpu.CompilerParams(vmem_limit_bytes=VMEM_LIMIT),
+            compiler_params=pltpu.CompilerParams(vmem_limit_bytes=limit),
             cost_estimate=pl.CostEstimate(flops=flops, bytes_accessed=moved, transcendentals=0),
         )(*operands)
 
@@ -77,14 +79,12 @@
 def pick_body(m_ref, s_ref, high_ref, low_ref):
     def step(j, carry):
         at = pl.ds(pl.multiple_of(j * ROWS, ROWS), ROWS)
-        rows = jnp.zeros((s_ref.shape[1], ROWS), F32)
+        rows = rest = jnp.zeros((s_ref.shape[1], ROWS), F32)
         for i in range(s_ref.shape[0]):
-            part = m_ref[i * ROWS:(i + 1) * ROWS, at]
-            high, low = halves(part)
-            tail = (part - high.astype(F32) - low.astype(F32)).astype(BF16)
+            high, low = halves(m_ref[i * ROWS:(i + 1) * ROWS, at])
             pick = s_ref[i]
-            rows = rows + (fast(pick, high) + fast(pick, low) + fast(pick, tail))
-        high_ref[:, at], low_ref[:, at] = halves(rows)
+            rows, rest = rows + fast(pick, high), rest + fast(pick, low)
+        high_ref[:, at], low_ref[:, at] = rows.astype(BF16), rest.astype(BF16)
         return carry
 
     lax.fori_loop(0, m_ref.shape[1] // ROWS, step, 0)
@@ -219,7 +219,21 @@
     return pair[:TILE] + pair[TILE:]
 
 
-def prepare_body(modes, group, gap_ref, coarse_ref, rigid_ref, s_ref, mate_ref, far_ref, wide_ref):
+def prepare_body(modes, group, gap_in_ref, coarse_in_ref, rigid_in_ref, s_ref, mate_ref, far_ref, wide_ref,
+                 gap_ref, coarse_raw_ref, rigid_raw_ref, coarse_ref, rigid_ref, sems):
+    loads = [
+        pltpu.make_async_copy(source_ref, target_ref, sems.at[number])
+        for number, (source_ref, target_ref) in enumerate(
+            ((gap_in_ref, gap_ref), (coarse_in_ref, coarse_raw_ref), (rigid_in_ref, rigid_raw_ref))
+        )
+    ]
+    for load in loads:
+        load.start()
+    for load in loads:
+        load.wait()
+    for source_ref, tile_ref in ((coarse_raw_ref, coarse_ref), (rigid_raw_ref, rigid_ref)):
+        tile_ref[...] = jnp.zeros_like(tile_ref)
+        tile_ref[:modes, :] = source_ref[...]
     shared = s_ref.shape[1] // 2
     cases = gap_ref.shape[1]
 
@@ -400,12 +414,20 @@
     def shaped(shape, dtype):
         return jax.ShapeDtypeStruct(shape, dtype)
 
-    pad = ((0, TILE - modes), (0, 0))
     payload = (shared + TILE * (outer * inner * TILE // cases) + TILE, cases)
     to_mate, to_far, rigid_wide = call(
         functools.partial(prepare_body, modes, inner),
-        [payload, payload, shaped((local_rows // ROWS, 2 * TILE, ROWS), BF16)], [], light, 8 * local_rows * cases,
-    )(gap_raw, jnp.pad(coarse_rows, pad), jnp.pad(rigid_images, pad), selector)
+        [payload, payload, shaped((local_rows // ROWS, 2 * TILE, ROWS), BF16)],
+        [
+            pltpu.VMEM(field, F32),
+            pltpu.VMEM(coarse_rows.shape, F32),
+            pltpu.VMEM(rigid_images.shape, F32),
+            pltpu.VMEM((TILE, coarse_rows.shape[1]), F32),
+            pltpu.VMEM((TILE, local_rows), F32),
+            pltpu.SemaphoreType.DMA((3,)),
+        ],
+        light, 8 * local_rows * cases, outside=3, limit=LARGE_LIMIT,
+    )(gap_raw, coarse_rows, rigid_images, selector)
     from_mate, from_far = exchanged(to_mate, to_far)
     edges = [
         call(pick_body, [shaped((2 * shared, local_rows), BF16)] * 2, [], light, 4 * local_rows * local_rows)(m, selector)

time: 215 us -> 215 us (level)
  transfers between devices with their start and end apart: 10 -> 10, of which waited for: 4 -> 4; matrix products, arithmetic and copies ran while one was open for 0% -> 0% of each run, Pallas kernels for 7% -> 6%
where the time goes in v3:
time: 215 us
  blocking collectives  151 us (70%)
  Pallas kernels  34.9 us (16%)
  starting transfers between devices  15.5 us (7%)
  waiting for transfers between devices  7.06 us (3%)
  local copies, waits for them, and re-layouts  3.45 us (2%)
    all_to_all x11, blocking collectives, swap(): return lax.all_to_all(blocks, axis, split_axis=0, concat_axis=0, tiled=True)  151 us
    pallas_call x22, Pallas kernels, run(): pl.pallas_call(body, out_shape=[s if hasattr(s, 'dtype') else jax.ShapeDt...  34.9 us
    ppermute x10, starting transfers between devices, matched(): return lax.ppermute(value, CLUSTER_SUB, pairs)  15.5 us
    ppermute x10, waiting for transfers between devices, matched(): return lax.ppermute(value, CLUSTER_SUB, pairs)  7.06 us
  transfers between devices with their start and end apart: 10, of which 4 were waited for; matrix products, arithmetic and copies ran while one was open for 0% of the time, Pallas kernels for 6%

profile of v3, /device:TPU:1, one launch (start us, length us, event | category | flops | bytes accessed | tf_op | source)
XLA Modules:
  0.0 214.7 jit_solution(1094833876242188854)
XLA Ops:
  0.7 0.8 fusion
  1.5 1.0 select_convert_fusion.1.s_ref
  2.4 4.7 %shard_map.85 = (f32[200,256]{1,0:T(8,128)}, f32[200,256]{1,0:T(8,128)}, bf16[4,16,256]{2,1,0:T(8,128)(2,1)}) custom-call(f32[1024,256]{1,0:T(8,128)} %y_ref.1, f32[6,1536]{1,0:T(8,128)} %coarse_in_ref.1, f32[6,1024]{1,0:T(8,128)} %rigid_in_ref.1, bf16[4,256,256]{2,1,0:T(8,128)(2,1)} %select_convert_fusion.1.s_ref), custom_call_target="tpu_custom_call" | custom-call | flops 268435456 | bytes 2097152 | tf_op jit(solution)/shard_map/pallas_call | solution.py:48
  7.1 0.0 copy-start
  7.1 3.1 %collective-permute-start.1 = (f32[200,256]{1,0:T(8,128)}, f32[200,256]{1,0:T(8,128)S(1)}, u32[]{:S(2)}, u32[]{:S(2)}) collective-permute-start(f32[200,256]{1,0:T(8,128)} %get-tuple-element.78), channel_id=1, source_target_pairs={{0,255},{1,2},{2,1},{3,4},{4,3},{5,6},{6,5},{7,8},{8,7},{9,10},{10... | collective-permute-start | bytes 614408 | tf_op jit(solution)/shard_map/ppermute | solution.py:37
  10.2 8.4 %collective-permute-start = (f32[200,256]{1,0:T(8,128)}, f32[200,256]{1,0:T(8,128)S(1)}, u32[]{:S(2)}, u32[]{:S(2)}) collective-permute-start(f32[200,256]{1,0:T(8,128)} %get-tuple-element.77.own_ref), channel_id=1, source_target_pairs={{0,1},{1,0},{2,3},{3,2},{4,5},{5,4},{6,7},{7,6},{8,9},{9,8},{10,11... | collective-permute-start | bytes 614408 | tf_op jit(solution)/shard_map/ppermute | solution.py:37
  18.7 0.2 select_reduce_fusion
  18.9 0.2 select_convert_fusion.st_ref.refs_3_
  19.1 0.0 copy-start.1
  19.1 2.2 %copy-done.1 = f32[1024,1024]{1,0:T(8,128)S(1)} copy-done((f32[1024,1024]{1,0:T(8,128)S(1)}, f32[1024,1024]{1,0:T(8,128)}, u32[]{:S(2)}) %copy-start.1) | copy-done | bytes 4194328
  21.3 1.0 copy-done.3
  22.3 1.8 shard_map.87
  24.1 0.0 copy-done
  24.1 0.0 copy-start.4
  24.1 1.8 shard_map.86
  26.0 0.0 collective-permute-done.1.far_ref
  26.0 0.0 collective-permute-done.mate_ref
  26.0 0.2 broadcast_in_dim.43.w_ref.refs_6_
  26.2 0.0 copy-done.6
  26.2 10.1 %all_to_all.55.block_ref = f32[16,24,128]{2,1,0:T(8,128)S(1)} all-to-all(f32[16,24,128]{2,1,0:T(8,128)S(1)} %shard_map.88), channel_id=1, replica_groups=mesh['cluster'=4,'sub_0'=4,'sub_1'=8,'sub_2'=2] {'cluster','sub_0'}, dimensions={0} | all-to-all | bytes 393216 | tf_op jit(solution)/shard_map/all_to_all | solution.py:33
  36.3 2.1 shard_map.89
  38.5 13.2 %all_to_all.56.near_ref = f32[16,8,256]{2,1,0:T(8,128)S(1)} all-to-all(f32[16,8,256]{2,1,0:T(8,128)S(1)} %get-tuple-element.97), channel_id=1, replica_groups=mesh['cluster'=4,'sub_0'=4,'sub_1'=8,'sub_2'=2] {'sub_1','sub_2'}, dimensions={0} | all-to-all | bytes 262144 | tf_op jit(solution)/shard_map/all_to_all | solution.py:33
  51.7 0.3 shard_map.90
  52.0 12.2 %all_to_all.57.near_ref = f32[16,24,256]{2,1,0:T(8,128)S(1)} all-to-all(f32[16,24,256]{2,1,0:T(8,128)S(1)} %shard_map.90), channel_id=1, replica_groups=mesh['cluster'=4,'sub_0'=4,'sub_1'=8,'sub_2'=2] {'cluster','sub_0'}, dimensions={0} | all-to-all | bytes 786432 | tf_op jit(solution)/shard_map/all_to_all | solution.py:33
  64.1 1.4 shard_map.91
  65.5 1.8 collective-permute-start.2
  67.3 0.3 collective-permute-start.3
  67.6 2.5 %shard_map.92 = (f32[1024,256]{1,0:T(8,128)S(1)}, f32[1,256]{1,0:T(1,128)S(1)}) custom-call(f32[1024,1024]{1,0:T(8,128)S(1)} %copy-done, f32[1024,256]{1,0:T(8,128)S(1)} %get-tuple-element.102.x_ref, bf16[1024,256]{1,0:T(8,128)(2,1)S(1)} %get-tuple-element.103.high_ref, bf16[1024,256]{1,0:T(8,128)(2,1)S(1)} %get-tuple-element.104.low_ref), custom_call_target="tpu_custom_call" | custom-call | flops 1610612736 | bytes 7340032 | tf_op jit(solution)/shard_map/pallas_call | solution.py:48
  70.1 0.0 copy-start.2
  70.2 0.0 collective-permute-done.2.refs_1_
  70.2 1.5 collective-permute-done.3.refs_2_
  71.7 1.8 shard_map.93
  73.5 17.1 %all_to_all.58.near_ref = f32[16,8,256]{2,1,0:T(8,128)S(1)} all-to-all(f32[16,8,256]{2,1,0:T(8,128)S(1)} %get-tuple-element.109), channel_id=1, replica_groups=mesh['cluster'=4,'sub_0'=4,'sub_1'=8,'sub_2'=2] {'sub_1','sub_2'}, dimensions={0} | all-to-all | bytes 262144 | tf_op jit(solution)/shard_map/all_to_all | solution.py:33
  90.6 0.3 shard_map.94
  90.9 13.1 %all_to_all.59.near_ref = f32[16,24,256]{2,1,0:T(8,128)S(1)} all-to-all(f32[16,24,256]{2,1,0:T(8,128)S(1)} %shard_map.94), channel_id=1, replica_groups=mesh['cluster'=4,'sub_0'=4,'sub_1'=8,'sub_2'=2] {'cluster','sub_0'}, dimensions={0} | all-to-all | bytes 786432 | tf_op jit(solution)/shard_map/all_to_all | solution.py:33
  104.0 1.4 shard_map.95
  105.4 0.6 collective-permute-start.4
  106.0 0.0 collective-permute-start.5
  106.0 2.5 %shard_map.96 = (f32[1024,256]{1,0:T(8,128)S(1)}, f32[1,256]{1,0:T(1,128)S(1)}) custom-call(f32[1024,1024]{1,0:T(8,128)S(1)} %copy-done.2, f32[1024,256]{1,0:T(8,128)S(1)} %get-tuple-element.113.x_ref.d_ref.first_ref, bf16[1024,256]{1,0:T(8,128)(2,1)S(1)} %get-tuple-element.114.high_ref, bf16[1024,256]{1,0:T(8,128)(2,1)S(1)} %get-tuple-element.115.low_ref), custom_call_target="tpu_custom_call" | custom-call | flops 1610612736 | bytes 7340032 | tf_op jit(solution)/shard_map/pallas_call | solution.py:48
  108.5 0.0 collective-permute-done.4.refs_1_
  108.5 1.8 collective-permute-done.5.refs_2_
  110.4 1.8 shard_map.97
  112.2 17.1 %all_to_all.60.near_ref = f32[16,8,256]{2,1,0:T(8,128)S(1)} all-to-all(f32[16,8,256]{2,1,0:T(8,128)S(1)} %get-tuple-element.120), channel_id=1, replica_groups=mesh['cluster'=4,'sub_0'=4,'sub_1'=8,'sub_2'=2] {'sub_1','sub_2'}, dimensions={0} | all-to-all | bytes 262144 | tf_op jit(solution)/shard_map/all_to_all | solution.py:33
  129.3 0.3 shard_map.98
  129.6 13.1 %all_to_all.61.near_ref = f32[16,24,256]{2,1,0:T(8,128)S(1)} all-to-all(f32[16,24,256]{2,1,0:T(8,128)S(1)} %shard_map.98), channel_id=1, replica_groups=mesh['cluster'=4,'sub_0'=4,'sub_1'=8,'sub_2'=2] {'cluster','sub_0'}, dimensions={0} | all-to-all | bytes 786432 | tf_op jit(solution)/shard_map/all_to_all | solution.py:33
  142.7 1.4 shard_map.99
  144.1 0.6 collective-permute-start.6
  144.7 0.0 collective-permute-start.7
  144.8 2.5 %shard_map.100 = (f32[1024,256]{1,0:T(8,128)S(1)}, f32[1,256]{1,0:T(1,128)S(1)}) custom-call(f32[1024,1024]{1,0:T(8,128)S(1)} %copy-done, f32[1024,256]{1,0:T(8,128)S(1)} %get-tuple-element.124.x_ref, bf16[1024,256]{1,0:T(8,128)(2,1)S(1)} %get-tuple-element.125.high_ref, bf16[1024,256]{1,0:T(8,128)(2,1)S(1)} %get-tuple-element.126.low_ref), custom_call_target="tpu_custom_call" | custom-call | flops 1610612736 | bytes 7340032 | tf_op jit(solution)/shard_map/pallas_call | solution.py:48
  147.3 0.0 collective-permute-done.6.refs_1_
  147.3 1.8 collective-permute-done.7.refs_2_
  149.1 1.8 shard_map.101
  151.0 17.3 %all_to_all.62.near_ref = f32[16,8,256]{2,1,0:T(8,128)S(1)} all-to-all(f32[16,8,256]{2,1,0:T(8,128)S(1)} %get-tuple-element.132), channel_id=1, replica_groups=mesh['cluster'=4,'sub_0'=4,'sub_1'=8,'sub_2'=2] {'sub_1','sub_2'}, dimensions={0} | all-to-all | bytes 262144 | tf_op jit(solution)/shard_map/all_to_all | solution.py:33
  168.3 0.3 shard_map.102
  168.5 13.1 %all_to_all.63.near_ref = f32[16,24,256]{2,1,0:T(8,128)S(1)} all-to-all(f32[16,24,256]{2,1,0:T(8,128)S(1)} %shard_map.102), channel_id=1, replica_groups=mesh['cluster'=4,'sub_0'=4,'sub_1'=8,'sub_2'=2] {'cluster','sub_0'}, dimensions={0} | all-to-all | bytes 786432 | tf_op jit(solution)/shard_map/all_to_all | solution.py:33
  181.7 1.4 shard_map.103
  183.1 0.6 collective-permute-start.8
  183.7 0.0 collective-permute-start.9
  183.7 2.5 %shard_map.104 = (f32[1024,256]{1,0:T(8,128)S(1)}, f32[16,1,256]{2,1,0:T(1,128)S(1)}) custom-call(f32[1024,1024]{1,0:T(8,128)S(1)} %copy-done.2, f32[1024,256]{1,0:T(8,128)S(1)} %get-tuple-element.134.x_ref.second_ref, bf16[1024,256]{1,0:T(8,128)(2,1)S(1)} %get-tuple-element.135.high_ref, bf16[1024,256]{1,0:T(8,128)(2,1)S(1)} %get-tuple-element.136.low_ref), custom_call_target="tpu_custom_call" | custom-call | flops 1610612736 | bytes 7340032 | tf_op jit(solution)/shard_map/pallas_call | solution.py:48
  186.2 0.0 collective-permute-done.8.mate_ref
  186.2 1.8 collective-permute-done.9.far_ref
  188.1 15.3 %all_to_all.64.near_ref = f32[16,1,256]{2,1,0:T(1,128)S(1)} all-to-all(f32[16,1,256]{2,1,0:T(1,128)S(1)} %get-tuple-element.147), channel_id=1, replica_groups=mesh['cluster'=4,'sub_0'=4,'sub_1'=8,'sub_2'=2] {'sub_1','sub_2'}, dimensions={0} | all-to-all | bytes 32768 | tf_op jit(solution)/shard_map/all_to_all | solution.py:33
  203.4 9.0 %all_to_all.65.bending_ref = f32[16,1,256]{2,1,0:T(1,128)S(1)} all-to-all(f32[16,1,256]{2,1,0:T(1,128)S(1)} %shard_map.105), channel_id=1, replica_groups=mesh['cluster'=4,'sub_0'=4,'sub_1'=8,'sub_2'=2] {'cluster','sub_0'}, dimensions={0} | all-to-all | bytes 32768 | tf_op jit(solution)/shard_map/all_to_all | solution.py:33
  212.4 2.4 %shard_map.106 = (f32[1024,256]{1,0:T(8,128)}, f32[1024,256]{1,0:T(8,128)}) custom-call(f32[1024,256]{1,0:T(8,128)S(1)} %get-tuple-element.137.q_ref, f32[128,256]{1,0:T(8,128)S(1)} %collective-permute-done.8.mate_ref, f32[128,256]{1,0:T(8,128)S(1)} %collective-permute-done.9.far_ref, bf16[1024,256]{1,0:T(8,128)(2,1)S(1)} %select_convert_fusion.st_ref.refs_3_, ...), custom_call_target="tpu_custom_call" | custom-call | flops 268435456 | bytes 6291456 | tf_op jit(solution)/shard_map/pallas_call | solution.py:48
  (13 shorter events, 0.1 us)
Async XLA Ops:
  7.1 17.0 %copy-start = (f32[1024,1024]{1,0:T(8,128)S(1)}, f32[1024,1024]{1,0:T(8,128)}, u32[]{:S(2)}) copy-start(f32[1024,1024]{1,0:T(8,128)} %m_ref.10) | copy-start | bytes 12582916
  7.1 18.8 %collective-permute-start.1 = (f32[200,256]{1,0:T(8,128)}, f32[200,256]{1,0:T(8,128)S(1)}, u32[]{:S(2)}, u32[]{:S(2)}) collective-permute-start(f32[200,256]{1,0:T(8,128)} %get-tuple-element.78), channel_id=1, source_target_pairs={{0,255},{1,2},{2,1},{3,4},{4,3},{5,6},{6,5},{7,8},{8,7},{9,10},{10... | collective-permute-start | bytes 614408 | tf_op jit(solution)/shard_map/ppermute | solution.py:37
  10.2 15.7 %collective-permute-start = (f32[200,256]{1,0:T(8,128)}, f32[200,256]{1,0:T(8,128)S(1)}, u32[]{:S(2)}, u32[]{:S(2)}) collective-permute-start(f32[200,256]{1,0:T(8,128)} %get-tuple-element.77.own_ref), channel_id=1, source_target_pairs={{0,1},{1,0},{2,3},{3,2},{4,5},{5,4},{6,7},{7,6},{8,9},{9,8},{10,11... | collective-permute-start | bytes 614408 | tf_op jit(solution)/shard_map/ppermute | solution.py:37
  19.1 2.2 %copy-start.1 = (f32[1024,1024]{1,0:T(8,128)S(1)}, f32[1024,1024]{1,0:T(8,128)}, u32[]{:S(2)}) copy-start(f32[1024,1024]{1,0:T(8,128)} %m_ref.11) | copy-start | bytes 12582916
  21.3 1.0 copy-start.3
  22.3 3.9 %copy-start.6 = (f32[200,256]{1,0:T(8,128)S(1)}, f32[200,256]{1,0:T(8,128)}, u32[]{:S(2)}) copy-start(f32[200,256]{1,0:T(8,128)} %get-tuple-element.77.own_ref) | copy-start | bytes 614404
  24.1 12.2 %copy-start.4 = (f32[1024,256]{1,0:T(8,128)S(1)}, f32[1024,256]{1,0:T(8,128)}, u32[]{:S(2)}) copy-start(f32[1024,256]{1,0:T(8,128)} %y_ref.1) | copy-start | bytes 3145732
  24.1 12.2 %copy-start.5 = (bf16[4,16,256]{2,1,0:T(8,128)(2,1)S(1)}, bf16[4,16,256]{2,1,0:T(8,128)(2,1)}, u32[]{:S(2)}) copy-start(bf16[4,16,256]{2,1,0:T(8,128)(2,1)} %get-tuple-element.96.wide_ref.refs_4_) | copy-start | bytes 98308
  65.5 4.6 %collective-permute-start.2 = (f32[128,256]{1,0:T(8,128)S(1)}, f32[128,256]{1,0:T(8,128)S(1)}, u32[]{:S(2)}, u32[]{:S(2)}) collective-permute-start(f32[128,256]{1,0:T(8,128)S(1)} %get-tuple-element.106), channel_id=1, source_target_pairs={{0,1},{1,0},{2,3},{3,2},{4,5},{5,4},{6,7},{7,6},{8,9},{9,8},{10,11... | collective-permute-start | bytes 393224 | tf_op jit(solution)/shard_map/ppermute | solution.py:37
  67.3 4.4 %collective-permute-start.3 = (f32[128,256]{1,0:T(8,128)S(1)}, f32[128,256]{1,0:T(8,128)S(1)}, u32[]{:S(2)}, u32[]{:S(2)}) collective-permute-start(f32[128,256]{1,0:T(8,128)S(1)} %get-tuple-element.107), channel_id=1, source_target_pairs={{0,255},{1,2},{2,1},{3,4},{4,3},{5,6},{6,5},{7,8},{8,7},{9,10},{10... | collective-permute-start | bytes 393224 | tf_op jit(solution)/shard_map/ppermute | solution.py:37
  70.1 35.9 %copy-start.2 = (f32[1024,1024]{1,0:T(8,128)S(1)}, f32[1024,1024]{1,0:T(8,128)}, u32[]{:S(2)}) copy-start(f32[1024,1024]{1,0:T(8,128)} %m_ref.11) | copy-start | bytes 12582916
  105.4 3.1 %collective-permute-start.4 = (f32[128,256]{1,0:T(8,128)S(1)}, f32[128,256]{1,0:T(8,128)S(1)}, u32[]{:S(2)}, u32[]{:S(2)}) collective-permute-start(f32[128,256]{1,0:T(8,128)S(1)} %get-tuple-element.117), channel_id=1, source_target_pairs={{0,1},{1,0},{2,3},{3,2},{4,5},{5,4},{6,7},{7,6},{8,9},{9,8},{10,11... | collective-permute-start | bytes 393224 | tf_op jit(solution)/shard_map/ppermute | solution.py:37
  106.0 4.4 %collective-permute-start.5 = (f32[128,256]{1,0:T(8,128)S(1)}, f32[128,256]{1,0:T(8,128)S(1)}, u32[]{:S(2)}, u32[]{:S(2)}) collective-permute-start(f32[128,256]{1,0:T(8,128)S(1)} %get-tuple-element.118), channel_id=1, source_target_pairs={{0,255},{1,2},{2,1},{3,4},{4,3},{5,6},{6,5},{7,8},{8,7},{9,10},{10... | collective-permute-start | bytes 393224 | tf_op jit(solution)/shard_map/ppermute | solution.py:37
  144.1 3.2 %collective-permute-start.6 = (f32[128,256]{1,0:T(8,128)S(1)}, f32[128,256]{1,0:T(8,128)S(1)}, u32[]{:S(2)}, u32[]{:S(2)}) collective-permute-start(f32[128,256]{1,0:T(8,128)S(1)} %get-tuple-element.128), channel_id=1, source_target_pairs={{0,1},{1,0},{2,3},{3,2},{4,5},{5,4},{6,7},{7,6},{8,9},{9,8},{10,11... | collective-permute-start | bytes 393224 | tf_op jit(solution)/shard_map/ppermute | solution.py:37
  144.7 4.4 %collective-permute-start.7 = (f32[128,256]{1,0:T(8,128)S(1)}, f32[128,256]{1,0:T(8,128)S(1)}, u32[]{:S(2)}, u32[]{:S(2)}) collective-permute-start(f32[128,256]{1,0:T(8,128)S(1)} %get-tuple-element.129), channel_id=1, source_target_pairs={{0,255},{1,2},{2,1},{3,4},{4,3},{5,6},{6,5},{7,8},{8,7},{9,10},{10... | collective-permute-start | bytes 393224 | tf_op jit(solution)/shard_map/ppermute | solution.py:37
  183.1 3.1 %collective-permute-start.8 = (f32[128,256]{1,0:T(8,128)S(1)}, f32[128,256]{1,0:T(8,128)S(1)}, u32[]{:S(2)}, u32[]{:S(2)}) collective-permute-start(f32[128,256]{1,0:T(8,128)S(1)} %get-tuple-element.140), channel_id=1, source_target_pairs={{0,1},{1,0},{2,3},{3,2},{4,5},{5,4},{6,7},{7,6},{8,9},{9,8},{10,11... | collective-permute-start | bytes 393224 | tf_op jit(solution)/shard_map/ppermute | solution.py:37
  183.7 4.4 %collective-permute-start.9 = (f32[128,256]{1,0:T(8,128)S(1)}, f32[128,256]{1,0:T(8,128)S(1)}, u32[]{:S(2)}, u32[]{:S(2)}) collective-permute-start(f32[128,256]{1,0:T(8,128)S(1)} %get-tuple-element.141), channel_id=1, source_target_pairs={{0,255},{1,2},{2,1},{3,4},{4,3},{5,6},{6,5},{7,8},{8,7},{9,10},{10... | collective-permute-start | bytes 393224 | tf_op jit(solution)/shard_map/ppermute | solution.py:37

commit v4 on v2

--- a/solution.py
+++ b/solution.py
@@ -77,14 +77,12 @@
 def pick_body(m_ref, s_ref, high_ref, low_ref):
     def step(j, carry):
         at = pl.ds(pl.multiple_of(j * ROWS, ROWS), ROWS)
-        rows = jnp.zeros((s_ref.shape[1], ROWS), F32)
+        rows = rest = jnp.zeros((s_ref.shape[1], ROWS), F32)
         for i in range(s_ref.shape[0]):
-            part = m_ref[i * ROWS:(i + 1) * ROWS, at]
-            high, low = halves(part)
-            tail = (part - high.astype(F32) - low.astype(F32)).astype(BF16)
+            high, low = halves(m_ref[i * ROWS:(i + 1) * ROWS, at])
             pick = s_ref[i]
-            rows = rows + (fast(pick, high) + fast(pick, low) + fast(pick, tail))
-        high_ref[:, at], low_ref[:, at] = halves(rows)
+            rows, rest = rows + fast(pick, high), rest + fast(pick, low)
+        high_ref[:, at], low_ref[:, at] = rows.astype(BF16), rest.astype(BF16)
         return carry
 
     lax.fori_loop(0, m_ref.shape[1] // ROWS, step, 0)

time: 215 us -> 213 us (level)
  transfers between devices with their start and end apart: 10 -> 10, of which waited for: 4 -> 4; matrix products, arithmetic and copies ran while one was open for 0% -> 0% of each run, Pallas kernels for 7% -> 6%
where the time goes in v4:
time: 213 us
  blocking collectives  151 us (71%)
  Pallas kernels  31.8 us (15%)
  starting transfers between devices  15.4 us (7%)
  waiting for transfers between devices  7.04 us (3%)
  local copies, waits for them, and re-layouts  5.43 us (3%)
    all_to_all x11, blocking collectives, swap(): return lax.all_to_all(blocks, axis, split_axis=0, concat_axis=0, tiled=True)  151 us
    pallas_call x22, Pallas kernels, run(): pl.pallas_call(body, out_shape=[s if hasattr(s, 'dtype') else jax.ShapeDt...  31.8 us
    ppermute x10, starting transfers between devices, matched(): return lax.ppermute(value, CLUSTER_SUB, pairs)  15.4 us
    ppermute x10, waiting for transfers between devices, matched(): return lax.ppermute(value, CLUSTER_SUB, pairs)  7.04 us
  transfers between devices with their start and end apart: 10, of which 4 were waited for; matrix products, arithmetic and copies ran while one was open for 0% of the time, Pallas kernels for 6%

profile of v4, /device:TPU:1, one launch (start us, length us, event | category | flops | bytes accessed | tf_op | source)
XLA Modules:
  0.0 212.8 jit_solution(8099149031411867433)
XLA Ops:
  0.7 0.8 pad.10.rigid_ref
  1.4 0.8 pad.9.coarse_ref
  2.3 0.9 fusion
  3.1 0.2 select_convert_fusion.1.s_ref
  3.3 0.0 copy-start.3
  3.3 1.4 copy-done.3
  4.8 1.6 shard_map.85
  6.4 3.0 %collective-permute-start.1 = (f32[200,256]{1,0:T(8,128)S(1)}, f32[200,256]{1,0:T(8,128)S(1)}, u32[]{:S(2)}, u32[]{:S(2)}) collective-permute-start(f32[200,256]{1,0:T(8,128)S(1)} %get-tuple-element.78), channel_id=1, source_target_pairs={{0,255},{1,2},{2,1},{3,4},{4,3},{5,6},{6,5},{7,8},{8,7},{9,10},{10... | collective-permute-start | bytes 614408 | tf_op jit(solution)/shard_map/ppermute | solution.py:36
  9.4 8.4 %collective-permute-start = (f32[200,256]{1,0:T(8,128)S(1)}, f32[200,256]{1,0:T(8,128)S(1)}, u32[]{:S(2)}, u32[]{:S(2)}) collective-permute-start(f32[200,256]{1,0:T(8,128)S(1)} %get-tuple-element.77.own_ref), channel_id=1, source_target_pairs={{0,1},{1,0},{2,3},{3,2},{4,5},{5,4},{6,7},{7,6},{8,9},{9,8},{10,11... | collective-permute-start | bytes 614408 | tf_op jit(solution)/shard_map/ppermute | solution.py:36
  17.8 0.2 select_reduce_fusion
  18.0 0.2 select_convert_fusion.st_ref.refs_3_
  18.2 0.0 copy-start.1
  18.2 2.2 %copy-done.1 = f32[1024,1024]{1,0:T(8,128)S(1)} copy-done((f32[1024,1024]{1,0:T(8,128)S(1)}, f32[1024,1024]{1,0:T(8,128)}, u32[]{:S(2)}) %copy-start.1) | copy-done | bytes 4194328
  20.4 1.8 shard_map.87
  22.2 0.0 copy-start.4
  22.2 1.8 shard_map.86
  24.1 0.0 collective-permute-done.1.far_ref
  24.1 0.0 collective-permute-done.mate_ref
  24.1 0.2 broadcast_in_dim.43.w_ref.refs_6_
  24.3 10.1 %all_to_all.55.block_ref = f32[16,24,128]{2,1,0:T(8,128)S(1)} all-to-all(f32[16,24,128]{2,1,0:T(8,128)S(1)} %shard_map.88), channel_id=1, replica_groups=mesh['cluster'=4,'sub_0'=4,'sub_1'=8,'sub_2'=2] {'cluster','sub_0'}, dimensions={0} | all-to-all | bytes 393216 | tf_op jit(solution)/shard_map/all_to_all | solution.py:32
  34.4 2.1 shard_map.89
  36.5 13.2 %all_to_all.56.near_ref = f32[16,8,256]{2,1,0:T(8,128)S(1)} all-to-all(f32[16,8,256]{2,1,0:T(8,128)S(1)} %get-tuple-element.97), channel_id=1, replica_groups=mesh['cluster'=4,'sub_0'=4,'sub_1'=8,'sub_2'=2] {'sub_1','sub_2'}, dimensions={0} | all-to-all | bytes 262144 | tf_op jit(solution)/shard_map/all_to_all | solution.py:32
  49.8 0.3 shard_map.90
  50.0 12.2 %all_to_all.57.near_ref = f32[16,24,256]{2,1,0:T(8,128)S(1)} all-to-all(f32[16,24,256]{2,1,0:T(8,128)S(1)} %shard_map.90), channel_id=1, replica_groups=mesh['cluster'=4,'sub_0'=4,'sub_1'=8,'sub_2'=2] {'cluster','sub_0'}, dimensions={0} | all-to-all | bytes 786432 | tf_op jit(solution)/shard_map/all_to_all | solution.py:32
  62.2 1.4 shard_map.91
  63.6 1.8 collective-permute-start.2
  65.4 0.3 collective-permute-start.3
  65.7 2.5 %shard_map.92 = (f32[1024,256]{1,0:T(8,128)S(1)}, f32[1,256]{1,0:T(1,128)S(1)}) custom-call(f32[1024,1024]{1,0:T(8,128)S(1)} %copy-done, f32[1024,256]{1,0:T(8,128)S(1)} %get-tuple-element.102.x_ref, bf16[1024,256]{1,0:T(8,128)(2,1)S(1)} %get-tuple-element.103.high_ref, bf16[1024,256]{1,0:T(8,128)(2,1)S(1)} %get-tuple-element.104.low_ref), custom_call_target="tpu_custom_call" | custom-call | flops 1610612736 | bytes 7340032 | tf_op jit(solution)/shard_map/pallas_call | solution.py:47
  68.2 0.0 copy-start.2
  68.2 0.0 collective-permute-done.2.refs_1_
  68.3 1.5 collective-permute-done.3.refs_2_
  69.8 1.8 shard_map.93
  71.6 17.1 %all_to_all.58.near_ref = f32[16,8,256]{2,1,0:T(8,128)S(1)} all-to-all(f32[16,8,256]{2,1,0:T(8,128)S(1)} %get-tuple-element.109), channel_id=1, replica_groups=mesh['cluster'=4,'sub_0'=4,'sub_1'=8,'sub_2'=2] {'sub_1','sub_2'}, dimensions={0} | all-to-all | bytes 262144 | tf_op jit(solution)/shard_map/all_to_all | solution.py:32
  88.7 0.3 shard_map.94
  89.0 13.1 %all_to_all.59.near_ref = f32[16,24,256]{2,1,0:T(8,128)S(1)} all-to-all(f32[16,24,256]{2,1,0:T(8,128)S(1)} %shard_map.94), channel_id=1, replica_groups=mesh['cluster'=4,'sub_0'=4,'sub_1'=8,'sub_2'=2] {'cluster','sub_0'}, dimensions={0} | all-to-all | bytes 786432 | tf_op jit(solution)/shard_map/all_to_all | solution.py:32
  102.1 1.4 shard_map.95
  103.5 0.6 collective-permute-start.4
  104.1 0.0 collective-permute-start.5
  104.1 2.5 %shard_map.96 = (f32[1024,256]{1,0:T(8,128)S(1)}, f32[1,256]{1,0:T(1,128)S(1)}) custom-call(f32[1024,1024]{1,0:T(8,128)S(1)} %copy-done.2, f32[1024,256]{1,0:T(8,128)S(1)} %get-tuple-element.113.x_ref.d_ref.first_ref, bf16[1024,256]{1,0:T(8,128)(2,1)S(1)} %get-tuple-element.114.high_ref, bf16[1024,256]{1,0:T(8,128)(2,1)S(1)} %get-tuple-element.115.low_ref), custom_call_target="tpu_custom_call" | custom-call | flops 1610612736 | bytes 7340032 | tf_op jit(solution)/shard_map/pallas_call | solution.py:47
  106.6 0.0 collective-permute-done.4.refs_1_
  106.6 1.8 collective-permute-done.5.refs_2_
  108.5 1.8 shard_map.97
  110.3 17.1 %all_to_all.60.near_ref = f32[16,8,256]{2,1,0:T(8,128)S(1)} all-to-all(f32[16,8,256]{2,1,0:T(8,128)S(1)} %get-tuple-element.120), channel_id=1, replica_groups=mesh['cluster'=4,'sub_0'=4,'sub_1'=8,'sub_2'=2] {'sub_1','sub_2'}, dimensions={0} | all-to-all | bytes 262144 | tf_op jit(solution)/shard_map/all_to_all | solution.py:32
  127.4 0.3 shard_map.98
  127.6 13.1 %all_to_all.61.near_ref = f32[16,24,256]{2,1,0:T(8,128)S(1)} all-to-all(f32[16,24,256]{2,1,0:T(8,128)S(1)} %shard_map.98), channel_id=1, replica_groups=mesh['cluster'=4,'sub_0'=4,'sub_1'=8,'sub_2'=2] {'cluster','sub_0'}, dimensions={0} | all-to-all | bytes 786432 | tf_op jit(solution)/shard_map/all_to_all | solution.py:32
  140.8 1.4 shard_map.99
  142.2 0.6 collective-permute-start.6
  142.8 0.0 collective-permute-start.7
  142.9 2.5 %shard_map.100 = (f32[1024,256]{1,0:T(8,128)S(1)}, f32[1,256]{1,0:T(1,128)S(1)}) custom-call(f32[1024,1024]{1,0:T(8,128)S(1)} %copy-done, f32[1024,256]{1,0:T(8,128)S(1)} %get-tuple-element.124.x_ref, bf16[1024,256]{1,0:T(8,128)(2,1)S(1)} %get-tuple-element.125.high_ref, bf16[1024,256]{1,0:T(8,128)(2,1)S(1)} %get-tuple-element.126.low_ref), custom_call_target="tpu_custom_call" | custom-call | flops 1610612736 | bytes 7340032 | tf_op jit(solution)/shard_map/pallas_call | solution.py:47
  145.4 0.0 collective-permute-done.6.refs_1_
  145.4 1.8 collective-permute-done.7.refs_2_
  147.2 1.8 shard_map.101
  149.0 17.3 %all_to_all.62.near_ref = f32[16,8,256]{2,1,0:T(8,128)S(1)} all-to-all(f32[16,8,256]{2,1,0:T(8,128)S(1)} %get-tuple-element.132), channel_id=1, replica_groups=mesh['cluster'=4,'sub_0'=4,'sub_1'=8,'sub_2'=2] {'sub_1','sub_2'}, dimensions={0} | all-to-all | bytes 262144 | tf_op jit(solution)/shard_map/all_to_all | solution.py:32
  166.3 0.3 shard_map.102
  166.6 13.1 %all_to_all.63.near_ref = f32[16,24,256]{2,1,0:T(8,128)S(1)} all-to-all(f32[16,24,256]{2,1,0:T(8,128)S(1)} %shard_map.102), channel_id=1, replica_groups=mesh['cluster'=4,'sub_0'=4,'sub_1'=8,'sub_2'=2] {'cluster','sub_0'}, dimensions={0} | all-to-all | bytes 786432 | tf_op jit(solution)/shard_map/all_to_all | solution.py:32
  179.7 1.4 shard_map.103
  181.2 0.6 collective-permute-start.8
  181.8 0.0 collective-permute-start.9
  181.8 2.5 %shard_map.104 = (f32[1024,256]{1,0:T(8,128)S(1)}, f32[16,1,256]{2,1,0:T(1,128)S(1)}) custom-call(f32[1024,1024]{1,0:T(8,128)S(1)} %copy-done.2, f32[1024,256]{1,0:T(8,128)S(1)} %get-tuple-element.134.x_ref.second_ref, bf16[1024,256]{1,0:T(8,128)(2,1)S(1)} %get-tuple-element.135.high_ref, bf16[1024,256]{1,0:T(8,128)(2,1)S(1)} %get-tuple-element.136.low_ref), custom_call_target="tpu_custom_call" | custom-call | flops 1610612736 | bytes 7340032 | tf_op jit(solution)/shard_map/pallas_call | solution.py:47
  184.3 0.0 collective-permute-done.8.mate_ref
  184.3 1.8 collective-permute-done.9.far_ref
  186.1 15.3 %all_to_all.64.near_ref = f32[16,1,256]{2,1,0:T(1,128)S(1)} all-to-all(f32[16,1,256]{2,1,0:T(1,128)S(1)} %get-tuple-element.147), channel_id=1, replica_groups=mesh['cluster'=4,'sub_0'=4,'sub_1'=8,'sub_2'=2] {'sub_1','sub_2'}, dimensions={0} | all-to-all | bytes 32768 | tf_op jit(solution)/shard_map/all_to_all | solution.py:32
  201.4 9.0 %all_to_all.65.bending_ref = f32[16,1,256]{2,1,0:T(1,128)S(1)} all-to-all(f32[16,1,256]{2,1,0:T(1,128)S(1)} %shard_map.105), channel_id=1, replica_groups=mesh['cluster'=4,'sub_0'=4,'sub_1'=8,'sub_2'=2] {'cluster','sub_0'}, dimensions={0} | all-to-all | bytes 32768 | tf_op jit(solution)/shard_map/all_to_all | solution.py:32
  210.4 2.4 %shard_map.106 = (f32[1024,256]{1,0:T(8,128)}, f32[1024,256]{1,0:T(8,128)}) custom-call(f32[1024,256]{1,0:T(8,128)S(1)} %get-tuple-element.137.q_ref, f32[128,256]{1,0:T(8,128)S(1)} %collective-permute-done.8.mate_ref, f32[128,256]{1,0:T(8,128)S(1)} %collective-permute-done.9.far_ref, bf16[1024,256]{1,0:T(8,128)(2,1)S(1)} %select_convert_fusion.st_ref.refs_3_, ...), custom_call_target="tpu_custom_call" | custom-call | flops 268435456 | bytes 6291456 | tf_op jit(solution)/shard_map/pallas_call | solution.py:47
  (11 shorter events, 0.1 us)
Async XLA Ops:
  2.2 20.0 %copy-start = (f32[1024,1024]{1,0:T(8,128)S(1)}, f32[1024,1024]{1,0:T(8,128)}, u32[]{:S(2)}) copy-start(f32[1024,1024]{1,0:T(8,128)} %m_ref.10) | copy-start | bytes 12582916
  3.3 1.5 copy-start.3
  6.4 17.7 %collective-permute-start.1 = (f32[200,256]{1,0:T(8,128)S(1)}, f32[200,256]{1,0:T(8,128)S(1)}, u32[]{:S(2)}, u32[]{:S(2)}) collective-permute-start(f32[200,256]{1,0:T(8,128)S(1)} %get-tuple-element.78), channel_id=1, source_target_pairs={{0,255},{1,2},{2,1},{3,4},{4,3},{5,6},{6,5},{7,8},{8,7},{9,10},{10... | collective-permute-start | bytes 614408 | tf_op jit(solution)/shard_map/ppermute | solution.py:36
  9.4 14.7 %collective-permute-start = (f32[200,256]{1,0:T(8,128)S(1)}, f32[200,256]{1,0:T(8,128)S(1)}, u32[]{:S(2)}, u32[]{:S(2)}) collective-permute-start(f32[200,256]{1,0:T(8,128)S(1)} %get-tuple-element.77.own_ref), channel_id=1, source_target_pairs={{0,1},{1,0},{2,3},{3,2},{4,5},{5,4},{6,7},{7,6},{8,9},{9,8},{10,11... | collective-permute-start | bytes 614408 | tf_op jit(solution)/shard_map/ppermute | solution.py:36
  18.2 2.2 %copy-start.1 = (f32[1024,1024]{1,0:T(8,128)S(1)}, f32[1024,1024]{1,0:T(8,128)}, u32[]{:S(2)}) copy-start(f32[1024,1024]{1,0:T(8,128)} %m_ref.11) | copy-start | bytes 12582916
  22.2 12.2 %copy-start.4 = (f32[1024,256]{1,0:T(8,128)S(1)}, f32[1024,256]{1,0:T(8,128)}, u32[]{:S(2)}) copy-start(f32[1024,256]{1,0:T(8,128)} %y_ref.1) | copy-start | bytes 3145732
  63.6 4.6 %collective-permute-start.2 = (f32[128,256]{1,0:T(8,128)S(1)}, f32[128,256]{1,0:T(8,128)S(1)}, u32[]{:S(2)}, u32[]{:S(2)}) collective-permute-start(f32[128,256]{1,0:T(8,128)S(1)} %get-tuple-element.106), channel_id=1, source_target_pairs={{0,1},{1,0},{2,3},{3,2},{4,5},{5,4},{6,7},{7,6},{8,9},{9,8},{10,11... | collective-permute-start | bytes 393224 | tf_op jit(solution)/shard_map/ppermute | solution.py:36
  65.4 4.4 %collective-permute-start.3 = (f32[128,256]{1,0:T(8,128)S(1)}, f32[128,256]{1,0:T(8,128)S(1)}, u32[]{:S(2)}, u32[]{:S(2)}) collective-permute-start(f32[128,256]{1,0:T(8,128)S(1)} %get-tuple-element.107), channel_id=1, source_target_pairs={{0,255},{1,2},{2,1},{3,4},{4,3},{5,6},{6,5},{7,8},{8,7},{9,10},{10... | collective-permute-start | bytes 393224 | tf_op jit(solution)/shard_map/ppermute | solution.py:36
  68.2 35.9 %copy-start.2 = (f32[1024,1024]{1,0:T(8,128)S(1)}, f32[1024,1024]{1,0:T(8,128)}, u32[]{:S(2)}) copy-start(f32[1024,1024]{1,0:T(8,128)} %m_ref.11) | copy-start | bytes 12582916
  103.5 3.2 %collective-permute-start.4 = (f32[128,256]{1,0:T(8,128)S(1)}, f32[128,256]{1,0:T(8,128)S(1)}, u32[]{:S(2)}, u32[]{:S(2)}) collective-permute-start(f32[128,256]{1,0:T(8,128)S(1)} %get-tuple-element.117), channel_id=1, source_target_pairs={{0,1},{1,0},{2,3},{3,2},{4,5},{5,4},{6,7},{7,6},{8,9},{9,8},{10,11... | collective-permute-start | bytes 393224 | tf_op jit(solution)/shard_map/ppermute | solution.py:36
  104.1 4.4 %collective-permute-start.5 = (f32[128,256]{1,0:T(8,128)S(1)}, f32[128,256]{1,0:T(8,128)S(1)}, u32[]{:S(2)}, u32[]{:S(2)}) collective-permute-start(f32[128,256]{1,0:T(8,128)S(1)} %get-tuple-element.118), channel_id=1, source_target_pairs={{0,255},{1,2},{2,1},{3,4},{4,3},{5,6},{6,5},{7,8},{8,7},{9,10},{10... | collective-permute-start | bytes 393224 | tf_op jit(solution)/shard_map/ppermute | solution.py:36
  142.2 3.2 %collective-permute-start.6 = (f32[128,256]{1,0:T(8,128)S(1)}, f32[128,256]{1,0:T(8,128)S(1)}, u32[]{:S(2)}, u32[]{:S(2)}) collective-permute-start(f32[128,256]{1,0:T(8,128)S(1)} %get-tuple-element.128), channel_id=1, source_target_pairs={{0,1},{1,0},{2,3},{3,2},{4,5},{5,4},{6,7},{7,6},{8,9},{9,8},{10,11... | collective-permute-start | bytes 393224 | tf_op jit(solution)/shard_map/ppermute | solution.py:36
  142.8 4.4 %collective-permute-start.7 = (f32[128,256]{1,0:T(8,128)S(1)}, f32[128,256]{1,0:T(8,128)S(1)}, u32[]{:S(2)}, u32[]{:S(2)}) collective-permute-start(f32[128,256]{1,0:T(8,128)S(1)} %get-tuple-element.129), channel_id=1, source_target_pairs={{0,255},{1,2},{2,1},{3,4},{4,3},{5,6},{6,5},{7,8},{8,7},{9,10},{10... | collective-permute-start | bytes 393224 | tf_op jit(solution)/shard_map/ppermute | solution.py:36
  181.2 3.1 %collective-permute-start.8 = (f32[128,256]{1,0:T(8,128)S(1)}, f32[128,256]{1,0:T(8,128)S(1)}, u32[]{:S(2)}, u32[]{:S(2)}) collective-permute-start(f32[128,256]{1,0:T(8,128)S(1)} %get-tuple-element.140), channel_id=1, source_target_pairs={{0,1},{1,0},{2,3},{3,2},{4,5},{5,4},{6,7},{7,6},{8,9},{9,8},{10,11... | collective-permute-start | bytes 393224 | tf_op jit(solution)/shard_map/ppermute | solution.py:36
  181.8 4.4 %collective-permute-start.9 = (f32[128,256]{1,0:T(8,128)S(1)}, f32[128,256]{1,0:T(8,128)S(1)}, u32[]{:S(2)}, u32[]{:S(2)}) collective-permute-start(f32[128,256]{1,0:T(8,128)S(1)} %get-tuple-element.141), channel_id=1, source_target_pairs={{0,255},{1,2},{2,1},{3,4},{4,3},{5,6},{6,5},{7,8},{8,7},{9,10},{10... | collective-permute-start | bytes 393224 | tf_op jit(solution)/shard_map/ppermute | solution.py:36
